TPU v7x, 32 devices: a whole 2x2x4 slice. The times are simulated.
32 devices in a mesh: member: 2 (over x), wide: 16 (over z, y, core).
Axes of the slice: x: 2, y: 2, z: 4, core: 2. Of those that a mesh axis runs over, the one named last changes fastest.
Arguments:
- stream_now: float32 [4, 256, 4096], P('member', 'wide'), parts along dimension 0, may hold values from -6 to 6
- vorticity: float32 [4, 256, 4096], P('member', 'wide'), parts along dimension 0, may hold values from -0.62 to 0.62
Outputs:
- vorticity_next: float32 [4, 256, 4096], P('member', 'wide'), parts along dimension 0
- stream_next: float32 [4, 256, 4096], P('member', 'wide'), parts along dimension 0
There are 2 independent parts, one for each index of `member`. A program takes and returns all parts, laid end to end along the dimension named above; each array names one. Nothing has to cross between parts.
All inputs are finite; a program needn't handle non-finite values.
Results may differ from a plain program's by a relative error of at most 0.00002.
Values sent between devices are 32-bit elements; how exact they have to be, the bound alone decides.
No kernel may reach another device: no remote copies, remote signals or barrier semaphores. Data moves between devices by JAX's collectives and lax.ppermute only.
A program may use at most 128 MiB of HBM per device.

v0:
```python
import jax
import jax.numpy as jnp
from jax import lax
from jax.sharding import PartitionSpec as P

LEVELS = 5
SWEEPS = 2
COARSE_SWEEPS = 8


relax_weight = 0.8
coupling_upper = 0.02
coupling_lower = 0.04
time_step = 0.5
beta_slope = 0.05
bottom_drag = 0.02


def extended(cells, sides, width):
    for axis, dim in sides:
        count = lax.axis_size(axis)
        ends = count - 1
        head = lax.slice_in_dim(cells, 0, width, axis=dim)
        tail = lax.slice_in_dim(cells, cells.shape[dim] - width, cells.shape[dim], axis=dim)
        cells = jnp.concatenate(
            [
                lax.ppermute(tail, axis, [(i, (i + 1) % count) for i in range(ends)]),
                cells,
                lax.ppermute(head, axis, [((i + 1) % count, i) for i in range(ends)]),
            ],
            axis=dim,
        )
    return cells


def coupling():
    return jnp.array([coupling_upper, coupling_lower], jnp.float32)[:, None, None]


def diagonal(spacing):
    return 4.0 / (spacing * spacing) + coupling()


def neighbours(padded):
    interior = padded[:, 1:-1, :]
    return (
        padded[:, 2:, :]
        + padded[:, :-2, :]
        + jnp.roll(interior, 1, axis=2)
        + jnp.roll(interior, -1, axis=2)
    )


def apply_operator(padded, spacing):
    interior = padded[:, 1:-1, :]
    return (4.0 * interior - neighbours(padded)) / (spacing * spacing) + coupling() * (
        interior - interior[::-1]
    )


def jacobi(padded, source, spacing):
    return padded[:, 1:-1, :] + relax_weight * (
        source - apply_operator(padded, spacing)
    ) / diagonal(spacing)


def shifted(padded, row_step, col_step):
    row_count = padded.shape[1] - 2
    return jnp.roll(padded[:, 1 + row_step : 1 + row_step + row_count, :], -col_step, axis=2)


def arakawa(stream_padded, vorticity_padded):

    def stream_at(row_step, col_step):
        return shifted(stream_padded, row_step, col_step)

    def vorticity_at(row_step, col_step):
        return shifted(vorticity_padded, row_step, col_step)

    first_form = (stream_at(0, 1) - stream_at(0, -1)) * (
        vorticity_at(1, 0) - vorticity_at(-1, 0)
    ) - (stream_at(1, 0) - stream_at(-1, 0)) * (vorticity_at(0, 1) - vorticity_at(0, -1))
    second_form = (
        stream_at(0, 1) * (vorticity_at(1, 1) - vorticity_at(-1, 1))
        - stream_at(0, -1) * (vorticity_at(1, -1) - vorticity_at(-1, -1))
        - stream_at(1, 0) * (vorticity_at(1, 1) - vorticity_at(1, -1))
        + stream_at(-1, 0) * (vorticity_at(-1, 1) - vorticity_at(-1, -1))
    )
    third_form = (
        vorticity_at(1, 0) * (stream_at(1, 1) - stream_at(1, -1))
        - vorticity_at(-1, 0) * (stream_at(-1, 1) - stream_at(-1, -1))
        - vorticity_at(0, 1) * (stream_at(1, 1) - stream_at(-1, 1))
        + vorticity_at(0, -1) * (stream_at(1, -1) - stream_at(-1, -1))
    )
    return (first_form + second_form + third_form) / 12.0


def advance(stream_padded, vorticity_padded, stream_now, vorticity):
    jacobian = arakawa(stream_padded, vorticity_padded)
    zonal_slope = (jnp.roll(stream_now, -1, axis=2) - jnp.roll(stream_now, 1, axis=2)) * 0.5
    drag_term = jnp.array([0.0, bottom_drag], jnp.float32)[:, None, None] * (
        neighbours(stream_padded) - 4.0 * stream_now
    )
    return vorticity - time_step * (jacobian + beta_slope * zonal_slope + drag_term)


def restrict(residual):
    return 0.25 * (
        residual[:, 0::2, 0::2]
        + residual[:, 1::2, 0::2]
        + residual[:, 0::2, 1::2]
        + residual[:, 1::2, 1::2]
    )


def prolong(correction):
    layers, row_count, col_count = correction.shape
    spread = jnp.broadcast_to(correction[:, :, None, :, None], (layers, row_count, 2, col_count, 2))
    return spread.reshape(layers, 2 * row_count, 2 * col_count)


def sweep_rims(iterate):
    return extended(iterate, (("wide", 1),), 1)


def relax(iterate, source, spacing, zero_start, with_residual):
    for sweep_index in range(SWEEPS):
        if zero_start and sweep_index == 0:
            iterate = relax_weight * source / diagonal(spacing)
        else:
            iterate = jacobi(sweep_rims(iterate), source, spacing)
    if with_residual:
        residual = source - apply_operator(sweep_rims(iterate), spacing)
        return (iterate, residual)
    return (iterate, source)


def coarse_solve(source, spacing):
    iterate = relax_weight * source / diagonal(spacing)
    for sweep_index in range(1, COARSE_SWEEPS):
        padded = extended(iterate, (("wide", 1),), 1)
        iterate = jacobi(padded, source, spacing)
    return iterate


def vcycle(grid_level, iterate, source, zero_start):
    spacing = 2.0**grid_level
    if grid_level == LEVELS - 1:
        return coarse_solve(source, spacing)
    iterate, residual = relax(iterate, source, spacing, zero_start, True)
    coarse_source = restrict(residual)
    correction = vcycle(grid_level + 1, jnp.zeros_like(coarse_source), coarse_source, True)
    iterate = iterate + prolong(correction)
    iterate, ignored = relax(iterate, source, spacing, False, False)
    return iterate


def shards(stream_now, vorticity):
    stacked = extended(jnp.stack([stream_now, vorticity]), (("wide", 2),), 1)
    vorticity_next = advance(stacked[0], stacked[1], stream_now, vorticity)
    stream_next = vcycle(0, stream_now, -vorticity_next, False)
    return (vorticity_next, stream_next)


def solution(mesh):
    return jax.shard_map(
        shards,
        mesh=mesh,
        in_specs=(P("member", "wide", None), P("member", "wide", None)),
        out_specs=(P("member", "wide", None), P("member", "wide", None)),
        check_vma=False,
    )
```

profile of v0, /device:TPU:8, one launch (start us, length us, event | category | flops | bytes accessed | tf_op | source)
XLA Modules:
  0.0 307.8 jit_solution(18191690101724934882)
XLA Ops:
  10.5 3.8 %collective-permute-start.1 = (f32[2,2,1,4096]{3,2,1,0:T(1,128)S(1)}, f32[2,2,1,4096]{3,2,1,0:T(1,128)S(1)}, u32[]{:S(2)}, u32[]{:S(2)}) collective-permute-start(f32[2,2,1,4096]{3,2,1,0:T(1,128)S(1)} %get-tuple-element.15), channel_id=1, source_target_pairs={{1,0},{2,1},{3,2},{4,3},{5,4},{6,5},{7,6},{8,7},{9,8},{10,9},{11,1... | collective-permute-start | bytes 196616 | tf_op jit(solution)/shard_map/ppermute | solution.py:29
  20.0 4.6 %collective-permute-start.4 = (f32[2,1,4096]{2,1,0:T(1,128)S(1)}, f32[2,1,4096]{2,1,0:T(1,128)S(1)}, u32[]{:S(2)}, u32[]{:S(2)}) collective-permute-start(f32[2,1,4096]{2,1,0:T(1,128)S(1)} %get-tuple-element.62), channel_id=1, source_target_pairs={{1,0},{2,1},{3,2},{4,3},{5,4},{6,5},{7,6},{8,7},{9,8},{10,9},{11,1... | collective-permute-start | bytes 98312 | tf_op jit(solution)/shard_map/ppermute | solution.py:29
  26.6 4.1 %collective-permute-done.5 = f32[2,1,4096]{2,1,0:T(1,128)S(1)} collective-permute-done((f32[2,1,4096]{2,1,0:T(1,128)S(1)}, f32[2,1,4096]{2,1,0:T(1,128)S(1)}, u32[]{:S(2)}, u32[]{:S(2)}) %collective-permute-start.5) | collective-permute-done | bytes 32800 | tf_op jit(solution)/shard_map/ppermute | solution.py:27
  39.9 4.4 %slice.840 = f32[2,8,2048]{2,1,0:T(8,128)S(1)} slice(f32[2,16,4096]{2,1,0:T(8,128)S(1)} %fusion.14), slice={[0:2:1], [1:16:2], [1:4096:2]} | slice | bytes 262144 | tf_op jit(solution)/shard_map/slice | solution.py:112
  44.3 4.4 %slice.839 = f32[2,8,2048]{2,1,0:T(8,128)S(1)} slice(f32[2,16,4096]{2,1,0:T(8,128)S(1)} %fusion.14), slice={[0:2:1], [0:16:2], [1:4096:2]} | slice | bytes 262144 | tf_op jit(solution)/shard_map/slice | solution.py:111
  48.7 4.6 %slice.838 = f32[2,8,2048]{2,1,0:T(8,128)S(1)} slice(f32[2,16,4096]{2,1,0:T(8,128)S(1)} %fusion.14), slice={[0:2:1], [1:16:2], [0:4096:2]} | slice | bytes 262144 | tf_op jit(solution)/shard_map/slice | solution.py:110
  53.2 4.4 %slice.837 = f32[2,8,2048]{2,1,0:T(8,128)S(1)} slice(f32[2,16,4096]{2,1,0:T(8,128)S(1)} %fusion.14), slice={[0:2:1], [0:16:2], [0:4096:2]} | slice | bytes 262144 | tf_op jit(solution)/shard_map/slice | solution.py:109
  62.3 3.5 %collective-permute-done.9 = f32[2,1,2048]{2,1,0:T(1,128)S(1)} collective-permute-done((f32[2,1,2048]{2,1,0:T(1,128)S(1)}, f32[2,1,2048]{2,1,0:T(1,128)S(1)}, u32[]{:S(2)}, u32[]{:S(2)}) %collective-permute-start.9) | collective-permute-done | bytes 16416 | tf_op jit(solution)/shard_map/ppermute | solution.py:27
  115.2 4.5 %collective-permute-start.20 = (f32[2,1,256]{2,1,0:T(1,128)S(1)}, f32[2,1,256]{2,1,0:T(1,128)S(1)}, u32[]{:S(2)}, u32[]{:S(2)}) collective-permute-start(f32[2,1,256]{2,1,0:T(1,128)S(1)} %get-tuple-element.2), channel_id=1, source_target_pairs={{1,0},{2,1},{3,2},{4,3},{5,4},{6,5},{7,6},{8,7},{9,8},{10,9},{11,1... | collective-permute-start | bytes 6152 | tf_op jit(solution)/shard_map/ppermute | solution.py:29
  123.1 4.5 %collective-permute-start.22 = (f32[2,1,256]{2,1,0:T(1,128)S(1)}, f32[2,1,256]{2,1,0:T(1,128)S(1)}, u32[]{:S(2)}, u32[]{:S(2)}) collective-permute-start(f32[2,1,256]{2,1,0:T(1,128)S(1)} %multiply_add_fusion.9), channel_id=1, source_target_pairs={{1,0},{2,1},{3,2},{4,3},{5,4},{6,5},{7,6},{8,7},{9,8},{10,9},{11,1... | collective-permute-start | bytes 6152 | tf_op jit(solution)/shard_map/ppermute | solution.py:29
  131.6 4.0 %collective-permute-start.24 = (f32[2,1,256]{2,1,0:T(1,128)S(1)}, f32[2,1,256]{2,1,0:T(1,128)S(1)}, u32[]{:S(2)}, u32[]{:S(2)}) collective-permute-start(f32[2,1,256]{2,1,0:T(1,128)S(1)} %multiply_add_fusion.8), channel_id=1, source_target_pairs={{1,0},{2,1},{3,2},{4,3},{5,4},{6,5},{7,6},{8,7},{9,8},{10,9},{11,1... | collective-permute-start | bytes 6152 | tf_op jit(solution)/shard_map/ppermute | solution.py:29
  139.5 4.0 %collective-permute-start.26 = (f32[2,1,256]{2,1,0:T(1,128)S(1)}, f32[2,1,256]{2,1,0:T(1,128)S(1)}, u32[]{:S(2)}, u32[]{:S(2)}) collective-permute-start(f32[2,1,256]{2,1,0:T(1,128)S(1)} %multiply_add_fusion.7), channel_id=1, source_target_pairs={{1,0},{2,1},{3,2},{4,3},{5,4},{6,5},{7,6},{8,7},{9,8},{10,9},{11,1... | collective-permute-start | bytes 6152 | tf_op jit(solution)/shard_map/ppermute | solution.py:29
  147.4 4.0 %collective-permute-start.28 = (f32[2,1,256]{2,1,0:T(1,128)S(1)}, f32[2,1,256]{2,1,0:T(1,128)S(1)}, u32[]{:S(2)}, u32[]{:S(2)}) collective-permute-start(f32[2,1,256]{2,1,0:T(1,128)S(1)} %multiply_add_fusion.6), channel_id=1, source_target_pairs={{1,0},{2,1},{3,2},{4,3},{5,4},{6,5},{7,6},{8,7},{9,8},{10,9},{11,1... | collective-permute-start | bytes 6152 | tf_op jit(solution)/shard_map/ppermute | solution.py:29
  155.3 4.0 %collective-permute-start.30 = (f32[2,1,256]{2,1,0:T(1,128)S(1)}, f32[2,1,256]{2,1,0:T(1,128)S(1)}, u32[]{:S(2)}, u32[]{:S(2)}) collective-permute-start(f32[2,1,256]{2,1,0:T(1,128)S(1)} %multiply_add_fusion.5), channel_id=1, source_target_pairs={{1,0},{2,1},{3,2},{4,3},{5,4},{6,5},{7,6},{8,7},{9,8},{10,9},{11,1... | collective-permute-start | bytes 6152 | tf_op jit(solution)/shard_map/ppermute | solution.py:29
  163.2 4.0 %collective-permute-start.32 = (f32[2,1,256]{2,1,0:T(1,128)S(1)}, f32[2,1,256]{2,1,0:T(1,128)S(1)}, u32[]{:S(2)}, u32[]{:S(2)}) collective-permute-start(f32[2,1,256]{2,1,0:T(1,128)S(1)} %multiply_add_fusion.4), channel_id=1, source_target_pairs={{1,0},{2,1},{3,2},{4,3},{5,4},{6,5},{7,6},{8,7},{9,8},{10,9},{11,1... | collective-permute-start | bytes 6152 | tf_op jit(solution)/shard_map/ppermute | solution.py:29
  169.1 4.5 %collective-permute-start.34 = (f32[2,1,512]{2,1,0:T(1,128)S(1)}, f32[2,1,512]{2,1,0:T(1,128)S(1)}, u32[]{:S(2)}, u32[]{:S(2)}) collective-permute-start(f32[2,1,512]{2,1,0:T(1,128)S(1)} %get-tuple-element.124), channel_id=1, source_target_pairs={{1,0},{2,1},{3,2},{4,3},{5,4},{6,5},{7,6},{8,7},{9,8},{10,9},{11,1... | collective-permute-start | bytes 12296 | tf_op jit(solution)/shard_map/ppermute | solution.py:29
  175.6 3.8 %collective-permute-done.35 = f32[2,1,512]{2,1,0:T(1,128)S(1)} collective-permute-done((f32[2,1,512]{2,1,0:T(1,128)S(1)}, f32[2,1,512]{2,1,0:T(1,128)S(1)}, u32[]{:S(2)}, u32[]{:S(2)}) %collective-permute-start.35) | collective-permute-done | bytes 4128 | tf_op jit(solution)/shard_map/ppermute | solution.py:27
  205.0 4.0 %broadcast_in_dim.19 = f32[2,4,2,1024,2]{4,3,2,1,0:T(8,128)} broadcast(f32[2,4,1024]{2,1,0:T(4,128)S(1)} %fusion.108), dimensions={0,1,3} | broadcast | bytes 163840 | tf_op jit(solution)/shard_map/broadcast_in_dim | solution.py:118
  209.0 8.7 %reshape.125 = f32[2,8,2048]{2,1,0:T(8,128)S(1)} reshape(f32[2,4,2,1024,2]{4,3,2,1,0:T(8,128)} %broadcast_in_dim.19) | data formatting | bytes 262144 | tf_op jit(solution)/shard_map/reshape | solution.py:119
  222.3 3.5 %collective-permute-done.43 = f32[2,1,2048]{2,1,0:T(1,128)S(1)} collective-permute-done((f32[2,1,2048]{2,1,0:T(1,128)S(1)}, f32[2,1,2048]{2,1,0:T(1,128)S(1)}, u32[]{:S(2)}, u32[]{:S(2)}) %collective-permute-start.43) | collective-permute-done | bytes 16416 | tf_op jit(solution)/shard_map/ppermute | solution.py:27
  234.1 11.4 %broadcast_in_dim.20 = f32[2,8,2,2048,2]{4,3,2,1,0:T(8,128)} broadcast(f32[2,8,2048]{2,1,0:T(8,128)S(1)} %fusion.67), dimensions={0,1,3} | broadcast | bytes 655360 | tf_op jit(solution)/shard_map/broadcast_in_dim | solution.py:118
  245.4 43.6 %reshape.126 = f32[2,16,4096]{2,1,0:T(8,128)S(1)} reshape(f32[2,8,2,2048,2]{4,3,2,1,0:T(8,128)} %broadcast_in_dim.20) | data formatting | bytes 1048576 | tf_op jit(solution)/shard_map/reshape | solution.py:119
  293.8 3.6 %collective-permute-done.47 = f32[2,1,4096]{2,1,0:T(1,128)S(1)} collective-permute-done((f32[2,1,4096]{2,1,0:T(1,128)S(1)}, f32[2,1,4096]{2,1,0:T(1,128)S(1)}, u32[]{:S(2)}, u32[]{:S(2)}) %collective-permute-start.47) | collective-permute-done | bytes 32800 | tf_op jit(solution)/shard_map/ppermute | solution.py:27
  302.5 3.6 %collective-permute-done.49 = f32[2,1,4096]{2,1,0:T(1,128)S(1)} collective-permute-done((f32[2,1,4096]{2,1,0:T(1,128)S(1)}, f32[2,1,4096]{2,1,0:T(1,128)S(1)}, u32[]{:S(2)}, u32[]{:S(2)}) %collective-permute-start.49) | collective-permute-done | bytes 32800 | tf_op jit(solution)/shard_map/ppermute | solution.py:27
  (223 shorter events, 156.3 us)
Async XLA Ops:
  1.8 16.0 %collective-permute-start.2 = (f32[2,1,4096]{2,1,0:T(1,128)S(1)}, f32[2,1,4096]{2,1,0:T(1,128)S(1)}, u32[]{:S(2)}, u32[]{:S(2)}) collective-permute-start(f32[2,1,4096]{2,1,0:T(1,128)S(1)} %get-tuple-element.68), channel_id=1, source_target_pairs={{1,0},{2,1},{3,2},{4,3},{5,4},{6,5},{7,6},{8,7},{9,8},{10,9},{11,1... | collective-permute-start | bytes 98312 | tf_op jit(solution)/shard_map/ppermute | solution.py:29
  4.5 13.2 %collective-permute-start.3 = (f32[2,1,4096]{2,1,0:T(1,128)S(1)}, f32[2,1,4096]{2,1,0:T(1,128)S(1)}, u32[]{:S(2)}, u32[]{:S(2)}) collective-permute-start(f32[2,1,4096]{2,1,0:T(1,128)S(1)} %get-tuple-element.69), channel_id=1, source_target_pairs={{0,1},{1,2},{2,3},{3,4},{4,5},{5,6},{6,7},{7,8},{8,9},{9,10},{10,1... | collective-permute-start | bytes 98312 | tf_op jit(solution)/shard_map/ppermute | solution.py:27
  7.8 6.8 %collective-permute-start = (f32[2,2,1,4096]{3,2,1,0:T(1,128)S(1)}, f32[2,2,1,4096]{3,2,1,0:T(1,128)S(1)}, u32[]{:S(2)}, u32[]{:S(2)}) collective-permute-start(f32[2,2,1,4096]{3,2,1,0:T(1,128)S(1)} %get-tuple-element.14), channel_id=1, source_target_pairs={{0,1},{1,2},{2,3},{3,4},{4,5},{5,6},{6,7},{7,8},{8,9},{9,10},{10,1... | collective-permute-start | bytes 196616 | tf_op jit(solution)/shard_map/ppermute | solution.py:27
  20.0 6.6 %collective-permute-start.4 = (f32[2,1,4096]{2,1,0:T(1,128)S(1)}, f32[2,1,4096]{2,1,0:T(1,128)S(1)}, u32[]{:S(2)}, u32[]{:S(2)}) collective-permute-start(f32[2,1,4096]{2,1,0:T(1,128)S(1)} %get-tuple-element.62), channel_id=1, source_target_pairs={{1,0},{2,1},{3,2},{4,3},{5,4},{6,5},{7,6},{8,7},{9,8},{10,9},{11,1... | collective-permute-start | bytes 98312 | tf_op jit(solution)/shard_map/ppermute | solution.py:29
  24.6 6.1 %collective-permute-start.5 = (f32[2,1,4096]{2,1,0:T(1,128)S(1)}, f32[2,1,4096]{2,1,0:T(1,128)S(1)}, u32[]{:S(2)}, u32[]{:S(2)}) collective-permute-start(f32[2,1,4096]{2,1,0:T(1,128)S(1)} %get-tuple-element.63), channel_id=1, source_target_pairs={{0,1},{1,2},{2,3},{3,4},{4,5},{5,6},{6,7},{7,8},{8,9},{9,10},{10,1... | collective-permute-start | bytes 98312 | tf_op jit(solution)/shard_map/ppermute | solution.py:27
  33.3 6.1 %collective-permute-start.7 = (f32[2,1,4096]{2,1,0:T(1,128)S(1)}, f32[2,1,4096]{2,1,0:T(1,128)S(1)}, u32[]{:S(2)}, u32[]{:S(2)}) collective-permute-start(f32[2,1,4096]{2,1,0:T(1,128)S(1)} %get-tuple-element.57), channel_id=1, source_target_pairs={{0,1},{1,2},{2,3},{3,4},{4,5},{5,6},{6,7},{7,8},{8,9},{9,10},{10,1... | collective-permute-start | bytes 98312 | tf_op jit(solution)/shard_map/ppermute | solution.py:27
  59.8 6.0 %collective-permute-start.9 = (f32[2,1,2048]{2,1,0:T(1,128)S(1)}, f32[2,1,2048]{2,1,0:T(1,128)S(1)}, u32[]{:S(2)}, u32[]{:S(2)}) collective-permute-start(f32[2,1,2048]{2,1,0:T(1,128)S(1)} %get-tuple-element.93), channel_id=1, source_target_pairs={{0,1},{1,2},{2,3},{3,4},{4,5},{5,6},{6,7},{7,8},{8,9},{9,10},{10,1... | collective-permute-start | bytes 49160 | tf_op jit(solution)/shard_map/ppermute | solution.py:27
  68.0 6.0 %collective-permute-start.11 = (f32[2,1,2048]{2,1,0:T(1,128)S(1)}, f32[2,1,2048]{2,1,0:T(1,128)S(1)}, u32[]{:S(2)}, u32[]{:S(2)}) collective-permute-start(f32[2,1,2048]{2,1,0:T(1,128)S(1)} %get-tuple-element.87), channel_id=1, source_target_pairs={{0,1},{1,2},{2,3},{3,4},{4,5},{5,6},{6,7},{7,8},{8,9},{9,10},{10,1... | collective-permute-start | bytes 49160 | tf_op jit(solution)/shard_map/ppermute | solution.py:27
  80.8 5.9 %collective-permute-start.13 = (f32[2,1,1024]{2,1,0:T(1,128)S(1)}, f32[2,1,1024]{2,1,0:T(1,128)S(1)}, u32[]{:S(2)}, u32[]{:S(2)}) collective-permute-start(f32[2,1,1024]{2,1,0:T(1,128)S(1)} %get-tuple-element.117), channel_id=1, source_target_pairs={{0,1},{1,2},{2,3},{3,4},{4,5},{5,6},{6,7},{7,8},{8,9},{9,10},{10,1... | collective-permute-start | bytes 24584 | tf_op jit(solution)/shard_map/ppermute | solution.py:27
  88.8 5.9 %collective-permute-start.15 = (f32[2,1,1024]{2,1,0:T(1,128)S(1)}, f32[2,1,1024]{2,1,0:T(1,128)S(1)}, u32[]{:S(2)}, u32[]{:S(2)}) collective-permute-start(f32[2,1,1024]{2,1,0:T(1,128)S(1)} %get-tuple-element.111), channel_id=1, source_target_pairs={{0,1},{1,2},{2,3},{3,4},{4,5},{5,6},{6,7},{7,8},{8,9},{9,10},{10,1... | collective-permute-start | bytes 24584 | tf_op jit(solution)/shard_map/ppermute | solution.py:27
  113.3 6.5 %collective-permute-start.21 = (f32[2,1,256]{2,1,0:T(1,128)S(1)}, f32[2,1,256]{2,1,0:T(1,128)S(1)}, u32[]{:S(2)}, u32[]{:S(2)}) collective-permute-start(f32[2,1,256]{2,1,0:T(1,128)S(1)} %get-tuple-element.2), channel_id=1, source_target_pairs={{0,1},{1,2},{2,3},{3,4},{4,5},{5,6},{6,7},{7,8},{8,9},{9,10},{10,1... | collective-permute-start | bytes 6152 | tf_op jit(solution)/shard_map/ppermute | solution.py:27
  121.2 6.5 %collective-permute-start.23 = (f32[2,1,256]{2,1,0:T(1,128)S(1)}, f32[2,1,256]{2,1,0:T(1,128)S(1)}, u32[]{:S(2)}, u32[]{:S(2)}) collective-permute-start(f32[2,1,256]{2,1,0:T(1,128)S(1)} %multiply_add_fusion.9), channel_id=1, source_target_pairs={{0,1},{1,2},{2,3},{3,4},{4,5},{5,6},{6,7},{7,8},{8,9},{9,10},{10,1... | collective-permute-start | bytes 6152 | tf_op jit(solution)/shard_map/ppermute | solution.py:27
  129.1 6.5 %collective-permute-start.25 = (f32[2,1,256]{2,1,0:T(1,128)S(1)}, f32[2,1,256]{2,1,0:T(1,128)S(1)}, u32[]{:S(2)}, u32[]{:S(2)}) collective-permute-start(f32[2,1,256]{2,1,0:T(1,128)S(1)} %multiply_add_fusion.8), channel_id=1, source_target_pairs={{0,1},{1,2},{2,3},{3,4},{4,5},{5,6},{6,7},{7,8},{8,9},{9,10},{10,1... | collective-permute-start | bytes 6152 | tf_op jit(solution)/shard_map/ppermute | solution.py:27
  137.0 6.5 %collective-permute-start.27 = (f32[2,1,256]{2,1,0:T(1,128)S(1)}, f32[2,1,256]{2,1,0:T(1,128)S(1)}, u32[]{:S(2)}, u32[]{:S(2)}) collective-permute-start(f32[2,1,256]{2,1,0:T(1,128)S(1)} %multiply_add_fusion.7), channel_id=1, source_target_pairs={{0,1},{1,2},{2,3},{3,4},{4,5},{5,6},{6,7},{7,8},{8,9},{9,10},{10,1... | collective-permute-start | bytes 6152 | tf_op jit(solution)/shard_map/ppermute | solution.py:27
  144.9 6.5 %collective-permute-start.29 = (f32[2,1,256]{2,1,0:T(1,128)S(1)}, f32[2,1,256]{2,1,0:T(1,128)S(1)}, u32[]{:S(2)}, u32[]{:S(2)}) collective-permute-start(f32[2,1,256]{2,1,0:T(1,128)S(1)} %multiply_add_fusion.6), channel_id=1, source_target_pairs={{0,1},{1,2},{2,3},{3,4},{4,5},{5,6},{6,7},{7,8},{8,9},{9,10},{10,1... | collective-permute-start | bytes 6152 | tf_op jit(solution)/shard_map/ppermute | solution.py:27
  152.9 6.5 %collective-permute-start.31 = (f32[2,1,256]{2,1,0:T(1,128)S(1)}, f32[2,1,256]{2,1,0:T(1,128)S(1)}, u32[]{:S(2)}, u32[]{:S(2)}) collective-permute-start(f32[2,1,256]{2,1,0:T(1,128)S(1)} %multiply_add_fusion.5), channel_id=1, source_target_pairs={{0,1},{1,2},{2,3},{3,4},{4,5},{5,6},{6,7},{7,8},{8,9},{9,10},{10,1... | collective-permute-start | bytes 6152 | tf_op jit(solution)/shard_map/ppermute | solution.py:27
  160.8 6.5 %collective-permute-start.33 = (f32[2,1,256]{2,1,0:T(1,128)S(1)}, f32[2,1,256]{2,1,0:T(1,128)S(1)}, u32[]{:S(2)}, u32[]{:S(2)}) collective-permute-start(f32[2,1,256]{2,1,0:T(1,128)S(1)} %multiply_add_fusion.4), channel_id=1, source_target_pairs={{0,1},{1,2},{2,3},{3,4},{4,5},{5,6},{6,7},{7,8},{8,9},{9,10},{10,1... | collective-permute-start | bytes 6152 | tf_op jit(solution)/shard_map/ppermute | solution.py:27
  169.1 6.5 %collective-permute-start.34 = (f32[2,1,512]{2,1,0:T(1,128)S(1)}, f32[2,1,512]{2,1,0:T(1,128)S(1)}, u32[]{:S(2)}, u32[]{:S(2)}) collective-permute-start(f32[2,1,512]{2,1,0:T(1,128)S(1)} %get-tuple-element.124), channel_id=1, source_target_pairs={{1,0},{2,1},{3,2},{4,3},{5,4},{6,5},{7,6},{8,7},{9,8},{10,9},{11,1... | collective-permute-start | bytes 12296 | tf_op jit(solution)/shard_map/ppermute | solution.py:29
  191.0 5.9 %collective-permute-start.39 = (f32[2,1,1024]{2,1,0:T(1,128)S(1)}, f32[2,1,1024]{2,1,0:T(1,128)S(1)}, u32[]{:S(2)}, u32[]{:S(2)}) collective-permute-start(f32[2,1,1024]{2,1,0:T(1,128)S(1)} %get-tuple-element.105), channel_id=1, source_target_pairs={{0,1},{1,2},{2,3},{3,4},{4,5},{5,6},{6,7},{7,8},{8,9},{9,10},{10,1... | collective-permute-start | bytes 24584 | tf_op jit(solution)/shard_map/ppermute | solution.py:27
  199.0 5.9 %collective-permute-start.41 = (f32[2,1,1024]{2,1,0:T(1,128)S(1)}, f32[2,1,1024]{2,1,0:T(1,128)S(1)}, u32[]{:S(2)}, u32[]{:S(2)}) collective-permute-start(f32[2,1,1024]{2,1,0:T(1,128)S(1)} %get-tuple-element.99), channel_id=1, source_target_pairs={{0,1},{1,2},{2,3},{3,4},{4,5},{5,6},{6,7},{7,8},{8,9},{9,10},{10,1... | collective-permute-start | bytes 24584 | tf_op jit(solution)/shard_map/ppermute | solution.py:27
  219.8 6.0 %collective-permute-start.43 = (f32[2,1,2048]{2,1,0:T(1,128)S(1)}, f32[2,1,2048]{2,1,0:T(1,128)S(1)}, u32[]{:S(2)}, u32[]{:S(2)}) collective-permute-start(f32[2,1,2048]{2,1,0:T(1,128)S(1)} %get-tuple-element.81), channel_id=1, source_target_pairs={{0,1},{1,2},{2,3},{3,4},{4,5},{5,6},{6,7},{7,8},{8,9},{9,10},{10,1... | collective-permute-start | bytes 49160 | tf_op jit(solution)/shard_map/ppermute | solution.py:27
  228.0 6.0 %collective-permute-start.45 = (f32[2,1,2048]{2,1,0:T(1,128)S(1)}, f32[2,1,2048]{2,1,0:T(1,128)S(1)}, u32[]{:S(2)}, u32[]{:S(2)}) collective-permute-start(f32[2,1,2048]{2,1,0:T(1,128)S(1)} %get-tuple-element.75), channel_id=1, source_target_pairs={{0,1},{1,2},{2,3},{3,4},{4,5},{5,6},{6,7},{7,8},{8,9},{9,10},{10,1... | collective-permute-start | bytes 49160 | tf_op jit(solution)/shard_map/ppermute | solution.py:27
  291.3 6.1 %collective-permute-start.47 = (f32[2,1,4096]{2,1,0:T(1,128)S(1)}, f32[2,1,4096]{2,1,0:T(1,128)S(1)}, u32[]{:S(2)}, u32[]{:S(2)}) collective-permute-start(f32[2,1,4096]{2,1,0:T(1,128)S(1)} %get-tuple-element.51), channel_id=1, source_target_pairs={{0,1},{1,2},{2,3},{3,4},{4,5},{5,6},{6,7},{7,8},{8,9},{9,10},{10,1... | collective-permute-start | bytes 98312 | tf_op jit(solution)/shard_map/ppermute | solution.py:27
  300.0 6.1 %collective-permute-start.49 = (f32[2,1,4096]{2,1,0:T(1,128)S(1)}, f32[2,1,4096]{2,1,0:T(1,128)S(1)}, u32[]{:S(2)}, u32[]{:S(2)}) collective-permute-start(f32[2,1,4096]{2,1,0:T(1,128)S(1)} %get-tuple-element.45), channel_id=1, source_target_pairs={{0,1},{1,2},{2,3},{3,4},{4,5},{5,6},{6,7},{7,8},{8,9},{9,10},{10,1... | collective-permute-start | bytes 98312 | tf_op jit(solution)/shard_map/ppermute | solution.py:27
  (36 other events, 560.4 us)
where the time goes:
time: 313 us; the launch traced here: 308 us
  starting transfers between devices  131 us (42%)
  local copies, waits for them, and re-layouts  101 us (32%)
  waiting for transfers between devices  65.5 us (21%)
  other arithmetic  8.23 us (3%)
    ppermute x25, starting transfers between devices, extended(): lax.ppermute(head, axis, [((i + 1) % count, i) for i in range(ends)])  71.6 us
    ppermute x25, starting transfers between devices, extended(): lax.ppermute(tail, axis, [(i, (i + 1) % count) for i in range(ends)])  59.1 us
    ppermute x25, waiting for transfers between devices, extended(): lax.ppermute(tail, axis, [(i, (i + 1) % count) for i in range(ends)])  55.3 us
    reshape x3, local copies, waits for them, and re-layouts, prolong(): return spread.reshape(layers, 2 * row_count, 2 * col_count)  53.6 us
    broadcast_in_dim x5, local copies, waits for them, and re-layouts, prolong(): jnp.broadcast_to(correction[:, :, None, :, None], (layers, row_count, 2,...  16 us
    ppermute x25, waiting for transfers between devices, extended(): lax.ppermute(head, axis, [((i + 1) % count, i) for i in range(ends)])  10.1 us
    slice x4, local copies, waits for them, and re-layouts, restrict(): residual[:, 1::2, 0::2]  6.32 us
  transfers between devices with their start and end apart: 50, of which 24 were waited for; matrix products, arithmetic and copies ran while one was open for 2% of the time, Pallas kernels for 0%

commit v1 on v0

v1 whole, which is shorter than its diff:
```python
import functools

import jax
import jax.numpy as jnp
from jax import lax
from jax.experimental import pallas as pl
from jax.experimental.pallas import tpu as pltpu
from jax.sharding import PartitionSpec as P


LANES = 128
SUBS = 8
HALO = 4
RELAX = 0.8
COUPLING = (0.02, 0.04)
TIME_STEP = 0.5
BETA = 0.05
DRAG = (0.0, 0.02)
COARSE_SWEEPS = 8


class Level:
    def __init__(self, level, tiles, stride):
        h2 = (2.0**level) ** 2
        self.tiles, self.stride = tiles, stride
        diag = [4.0 / h2 + f for f in COUPLING]
        self.keep = 1.0 - RELAX
        self.near = [RELAX / (d * h2) for d in diag]
        self.other = [RELAX * f / d for f, d in zip(COUPLING, diag)]
        self.src = [RELAX / d for d in diag]
        self.diag = diag
        self.inv_h2 = 1.0 / h2
        self.size = tiles * SUBS


def lane_index():
    return lax.broadcasted_iota(jnp.int32, (SUBS, LANES), 1)


def at(level, row, tile=0):
    base = row * level.size
    if not isinstance(row, int):
        base = pl.multiple_of(base, SUBS)
    return pl.ds(base + tile * SUBS, SUBS)


def load(ref, level, layer, row):
    return [ref[layer, at(level, row, t), :] for t in range(level.tiles)]


def store(ref, level, layer, row, values):
    for t in range(level.tiles):
        ref[layer, at(level, row, t), :] = values[t]


def east(values, stride=1):
    rolled = [pltpu.roll(v, LANES - stride, 1) for v in values]
    after = rolled[1:] + [pltpu.roll(rolled[0], SUBS - 1, 0)]
    edge = lane_index() >= LANES - stride
    return [jnp.where(edge, a, r) for a, r in zip(after, rolled)]


def west(values, stride=1):
    rolled = [pltpu.roll(v, stride, 1) for v in values]
    before = [pltpu.roll(rolled[-1], 1, 0)] + rolled[:-1]
    edge = lane_index() < stride
    return [jnp.where(edge, b, r) for b, r in zip(before, rolled)]


def row_blocks(low, high, block, body):
    count = high - low if isinstance(low, int) else high
    whole = count // block
    if whole > 1:
        lax.fori_loop(0, whole, lambda i, c: (body(low + i * block, block), c)[1], 0)
    elif whole == 1:
        body(low, block)
    if count % block:
        body(low + whole * block, count % block)


def star(rows, k, layer, level):
    centre = rows[k][layer]
    e, w = east(centre, level.stride), west(centre, level.stride)
    return [
        (n + s) + (a + b)
        for n, s, a, b in zip(rows[k + 1][layer], rows[k - 1][layer], e, w)
    ]


def load_rows(ref, level, first, count, margin=1):
    return {
        k: [load(ref, level, layer, first + k) for layer in range(2)]
        for k in range(-margin, count + margin)
    }


def sweep_rows(level, rows, source, count):
    out = {}
    for k in range(count):
        out[k] = []
        for layer in range(2):
            near = star(rows, k, layer, level)
            out[k].append(
                [
                    (level.keep * c + level.near[layer] * n)
                    + (level.other[layer] * o + level.src[layer] * b)
                    for c, n, o, b in zip(
                        rows[k][layer], near, rows[k][1 - layer], source[k][layer]
                    )
                ]
            )
    return out


def residual_rows(level, rows, source, count):
    out = {}
    for k in range(count):
        out[k] = []
        for layer in range(2):
            near = star(rows, k, layer, level)
            out[k].append(
                [
                    (b - level.diag[layer] * c)
                    + (level.inv_h2 * n + COUPLING[layer] * o)
                    for c, n, o, b in zip(
                        rows[k][layer], near, rows[k][1 - layer], source[k][layer]
                    )
                ]
            )
    return out


def store_rows(ref, level, first, rows, count):
    for k in range(count):
        for layer in range(2):
            store(ref, level, layer, first + k, rows[k][layer])


def sweep(level, dst, dst_at, src, src_at, b, b_at, low, high, block):
    def body(first, count):
        rows = load_rows(src, level, first + src_at, count)
        source = load_rows(b, level, first + b_at, count, 0)
        store_rows(dst, level, first + dst_at, sweep_rows(level, rows, source, count), count)

    row_blocks(low, high, block, body)


def start(level, dst, dst_at, b, b_at, low, high, block):
    def body(first, count):
        source = load_rows(b, level, first + b_at, count, 0)
        out = {
            k: [[level.src[l] * x for x in source[k][l]] for l in range(2)]
            for k in range(count)
        }
        store_rows(dst, level, first + dst_at, out, count)

    row_blocks(low, high, block, body)


def pack_columns(values):
    lane = lane_index()
    pick = (2 * lane) % LANES
    sums = [v + pltpu.roll(v, LANES - 1, 1) for v in values]
    picked = [jnp.take_along_axis(s, pick, axis=1) for s in sums]
    return [
        jnp.where(lane < LANES // 2, picked[2 * t], picked[2 * t + 1])
        for t in range(len(values) // 2)
    ]


def spread_columns(values):
    lane = lane_index()
    out = []
    for v in values:
        out.append(jnp.take_along_axis(v, lane // 2, axis=1))
        out.append(jnp.take_along_axis(v, LANES // 2 + lane // 2, axis=1))
    return out


def merge_columns(values, stride):
    even = (lane_index() // stride) % 2 == 0
    return [
        v + jnp.where(even, pltpu.roll(v, LANES - stride, 1), pltpu.roll(v, stride, 1))
        for v in values
    ]


def restrict(fine, dst, dst_at, coarse, src, src_at, b, b_at, low, high, block):
    def body(first, count):
        rows = load_rows(src, fine, 2 * first + src_at, 2 * count)
        source = load_rows(b, fine, 2 * first + b_at, 2 * count, 0)
        res = residual_rows(fine, rows, source, 2 * count)
        out = {}
        for k in range(count):
            out[k] = []
            for layer in range(2):
                pair = [x + y for x, y in zip(res[2 * k][layer], res[2 * k + 1][layer])]
                if coarse.tiles < fine.tiles:
                    pair = pack_columns(pair)
                else:
                    pair = merge_columns(pair, fine.stride)
                out[k].append([0.25 * x for x in pair])
        store_rows(dst, coarse, first + dst_at, out, count)

    row_blocks(low, high, block, body)


def correct(fine, coarse, dst, dst_at, src, src_at, add, add_at, low, high, block):
    def body(first, count):
        coarse_rows = load_rows(add, coarse, first + add_at, count, 0)
        fine_rows = load_rows(src, fine, 2 * first + src_at, 2 * count, 0)
        out = {}
        for k in range(count):
            spread = [
                spread_columns(v) if coarse.tiles < fine.tiles else v for v in coarse_rows[k]
            ]
            for half in range(2):
                out[2 * k + half] = [
                    [x + y for x, y in zip(fine_rows[2 * k + half][l], spread[l])]
                    for l in range(2)
                ]
        store_rows(dst, fine, 2 * first + dst_at, out, 2 * count)

    row_blocks(low, high, block, body)


def clear(ref, level, low, high):
    ref[:, low * level.size : high * level.size, :] = jnp.zeros(
        (ref.shape[0], (high - low) * level.size, LANES), jnp.float32
    )


def place():
    me, count = lax.axis_index("wide"), lax.axis_size("wide")
    return me, lax.rem(me, 2), me == 0, me == count - 1


def to_native(dst, src, level, src_at, rows):
    for layer in range(2):
        for group in range(rows // SUBS):
            for t in range(level.tiles):
                for s in range(SUBS):
                    first = (src_at + group * SUBS) * level.size + t * SUBS + s
                    column = (s * level.tiles + t) * LANES
                    dst[layer, group * SUBS : (group + 1) * SUBS, column : column + LANES] = src[
                        layer, pl.ds(first, SUBS, stride=level.size), :
                    ]


def pack_kernel(level, rows, p_ref, q_ref, x_ref, near_ref, far_ref):
    for field, ref in enumerate((p_ref, q_ref)):
        for layer in range(2):
            for group in range(rows // SUBS):
                for t in range(level.tiles):
                    for s in range(SUBS):
                        first = group * SUBS * level.size + t * SUBS + s
                        column = (s * level.tiles + t) * LANES
                        x_ref[2 * field + layer, pl.ds(first, SUBS, stride=level.size), :] = ref[
                            layer, group * SUBS : (group + 1) * SUBS, column : column + LANES
                        ]
    send_edges(level, rows, x_ref, 0, near_ref, far_ref)


def send_edges(level, rows, src, src_at, near_ref, far_ref):
    _, odd, _, _ = place()
    size = HALO * level.size
    last = (src_at + rows - HALO) * level.size
    top = src_at * level.size
    near = pl.multiple_of(jnp.where(odd == 1, top, last), SUBS)
    far = pl.multiple_of(jnp.where(odd == 1, last, top), SUBS)
    near_ref[...] = src[:, pl.ds(near, size), :]
    far_ref[...] = src[:, pl.ds(far, size), :]


def join(level, rows, dst, own, near_ref, far_ref):
    _, odd, first, last = place()
    size = HALO * level.size
    low = (HALO + rows) * level.size
    near = pl.multiple_of(jnp.where(odd == 1, 0, low), SUBS)
    far = pl.multiple_of(jnp.where(odd == 1, low, 0), SUBS)
    dst[:, size : size + rows * level.size, :] = own[...]
    dst[:, pl.ds(near, size), :] = near_ref[...]
    outside = jnp.logical_or(first, last)
    dst[:, pl.ds(far, size), :] = jnp.where(outside, 0.0, far_ref[...])


def fine_kernel(
    level, coarse, rows, x_ref, near_ref, far_ref,
    next_ref, b_ref, v_ref, bc_ref, bc_near_ref, bc_far_ref,
    ext, e_ref, w_ref, b_all, v_one,
):
    _, _, is_first, is_last = place()
    total = rows + 2 * HALO
    join(level, rows, ext, x_ref, near_ref, far_ref)

    def shift_body(first, count):
        for k in range(count):
            for f in range(4):
                v = load(ext, level, f, first + k)
                store(e_ref, level, f, first + k, east(v))
                store(w_ref, level, f, first + k, west(v))

    row_blocks(0, total, 2, shift_body)

    def advance_body(first, count):
        for layer in range(2):
            for t in range(level.tiles):
                def grab(ref, field):
                    return {
                        k: ref[2 * field + layer, at(level, first + k, t), :]
                        for k in range(-1, count + 1)
                    }

                p, pe, pw = grab(ext, 0), grab(e_ref, 0), grab(w_ref, 0)
                q, qe, qw = grab(ext, 1), grab(e_ref, 1), grab(w_ref, 1)
                zonal = {k: pe[k] - pw[k] for k in p}
                for k in range(count):
                    n, s = k + 1, k - 1
                    v0, ve, vw = p[n] - p[s], pe[n] - pe[s], pw[n] - pw[s]
                    jac = q[n] * (zonal[k] + zonal[n]) - q[s] * (zonal[k] + zonal[s])
                    jac = jac - qe[k] * (v0 + ve) + qw[k] * (v0 + vw)
                    jac = jac + qe[n] * (pe[k] - p[n]) - qe[s] * (pe[k] - p[s])
                    jac = jac - qw[n] * (pw[k] - p[n]) + qw[s] * (pw[k] - p[s])
                    step = (TIME_STEP / 12.0) * jac + (0.5 * TIME_STEP * BETA) * zonal[k]
                    if layer == 1:
                        lap = (p[n] + p[s]) + (pe[k] + pw[k]) - 4.0 * p[k]
                        step = step + (TIME_STEP * DRAG[1]) * lap
                    b_all[layer, at(level, first + k, t), :] = step - q[k]

    row_blocks(1, total - 1, 2, advance_body)

    sweep(level, v_one, 0, ext, 0, b_all, 0, 1, total - 1, 2)

    @pl.when(is_first)
    def _():
        clear(v_one, level, 0, HALO)

    @pl.when(is_last)
    def _():
        clear(v_one, level, HALO + rows, total)

    sweep(level, v_ref, -2, v_one, 0, b_all, 0, 2, total - 2, 2)

    @pl.when(is_first)
    def _():
        clear(v_ref, level, 0, 2)

    @pl.when(is_last)
    def _():
        clear(v_ref, level, rows + 2, rows + 4)

    restrict(level, bc_ref, 0, coarse, v_ref, 2, b_all, HALO, 0, rows // 2, 1)
    send_edges(coarse, rows // 2, bc_ref, 0, bc_near_ref, bc_far_ref)
    b_ref[...] = b_all[:, 3 * level.size : (total - 3) * level.size, :]
    for layer in range(2):
        for group in range(rows // SUBS):
            for t in range(level.tiles):
                for s in range(SUBS):
                    first = (HALO + group * SUBS) * level.size + t * SUBS + s
                    column = (s * level.tiles + t) * LANES
                    next_ref[
                        layer, group * SUBS : (group + 1) * SUBS, column : column + LANES
                    ] = -b_all[layer, pl.ds(first, SUBS, stride=level.size), :]


def middle_kernel(
    level, coarse, rows, b_own, near_ref, far_ref, b_ref, v_ref, out_ref, v_one, bc
):
    _, _, is_first, is_last = place()
    total = rows + 2 * HALO
    join(level, rows, b_ref, b_own, near_ref, far_ref)
    start(level, v_one, 0, b_ref, 0, 0, total, 4)

    @pl.when(is_first)
    def _():
        clear(v_one, level, 0, HALO)

    @pl.when(is_last)
    def _():
        clear(v_one, level, HALO + rows, total)

    sweep(level, v_ref, 0, v_one, 0, b_ref, 0, 1, total - 1, 2)

    @pl.when(is_first)
    def _():
        clear(v_ref, level, 0, HALO)

    @pl.when(is_last)
    def _():
        clear(v_ref, level, HALO + rows, total)

    restrict(level, bc, 0, coarse, v_ref, HALO, b_ref, HALO, 0, rows // 2, 2)
    for copy in range(out_ref.shape[0]):
        out_ref[copy] = bc[...]


PAD = 4


def coarse_kernel(
    levels, rows, same_ref, other_ref, b1_ref, v1_ref, b0_ref, v0_ref, out_ref,
    b2, v2, w2, b3, v3, w3, b4, v4, w4, x1, y1, x0, y0,
):
    me, odd, is_first, is_last = place()
    fine, mid, two, three, four = levels
    own = rows // 4
    chips = same_ref.shape[0]
    n2, n3, n4 = 2 * chips * own, chips * own, chips * own // 2
    for ref, level, n in (
        (b2, two, n2), (v2, two, n2), (w2, two, n2), (b3, three, n3), (v3, three, n3),
        (w3, three, n3), (v4, four, n4), (w4, four, n4),
    ):
        clear(ref, level, 0, PAD)
        clear(ref, level, PAD + n, 2 * PAD + n)

    def gather_body(chip, carry):
        for ref, core in ((same_ref, odd), (other_ref, 1 - odd)):
            row = pl.multiple_of(((2 * chip + core) * own + PAD) * two.size, SUBS)
            b2[:, pl.ds(row, own * two.size), :] = ref[chip]
        return carry

    lax.fori_loop(0, chips, gather_body, 0, unroll=min(chips, 4))

    start(two, v2, PAD, b2, PAD, 0, n2, 8)
    sweep(two, w2, PAD, v2, PAD, b2, PAD, 0, n2, 8)
    restrict(two, b3, PAD, three, w2, PAD, b2, PAD, 0, n3, 4)
    start(three, v3, PAD, b3, PAD, 0, n3, 8)
    sweep(three, w3, PAD, v3, PAD, b3, PAD, 0, n3, 8)
    restrict(three, b4, 0, four, w3, PAD, b3, PAD, 0, n4, 4)
    start(four, v4, PAD, b4, 0, 0, n4, 8)
    src, dst = v4, w4
    for _ in range(COARSE_SWEEPS - 1):
        sweep(four, dst, PAD, src, PAD, b4, 0, 0, n4, 16)
        src, dst = dst, src

    def trim(ref, level, n):
        @pl.when(me < 2)
        def _():
            clear(ref, level, 0, PAD)

        @pl.when(me >= 2 * chips - 2)
        def _():
            clear(ref, level, PAD + n, 2 * PAD + n)

    half, quarter = own // 2, own // 4
    correct(three, four, v3, PAD, w3, PAD, src, PAD, me * quarter - 2, quarter + 4, 8)
    sweep(three, w3, PAD, v3, PAD, b3, PAD, me * half - 3, half + 6, 8)
    trim(w3, three, n3)
    sweep(three, v3, PAD, w3, PAD, b3, PAD, me * half - 2, half + 4, 8)
    trim(v3, three, n3)
    correct(two, three, v2, PAD, w2, PAD, v3, PAD, me * half - 2, half + 4, 8)
    sweep(two, w2, PAD, v2, PAD, b2, PAD, me * own - 3, own + 6, 8)
    trim(w2, two, n2)
    sweep(two, v2, PAD, w2, PAD, b2, PAD, me * own - 2, own + 4, 8)
    trim(v2, two, n2)

    n1 = rows // 2
    total = n1 + 2 * HALO

    def trim_own(ref, level, halo, n):
        @pl.when(is_first)
        def _():
            clear(ref, level, 0, halo)

        @pl.when(is_last)
        def _():
            clear(ref, level, halo + n, 2 * halo + n)

    correct(
        mid, two, x1, 0, v1_ref, 0, v2, PAD + me * own - HALO // 2, 0, total // 2, 2
    )
    sweep(mid, y1, 0, x1, 0, b1_ref, 0, 2, total - 2, 2)
    trim_own(y1, mid, HALO, n1)
    sweep(mid, x1, 0, y1, 0, b1_ref, 0, 3, total - 3, 2)
    trim_own(x1, mid, HALO, n1)

    correct(fine, mid, x0, 0, v0_ref, 0, x1, HALO - 1, 0, n1 + 2, 1)
    sweep(fine, y0, 0, x0, 0, b0_ref, -1, 1, rows + 3, 2)
    trim_own(y0, fine, 2, rows)
    sweep(fine, x0, 0, y0, 0, b0_ref, -1, 2, rows + 2, 2)
    to_native(out_ref, x0, fine, 2, rows)


def shape(*dims):
    return jax.ShapeDtypeStruct(dims, jnp.float32)


def scratch(layers, rows, level):
    return pltpu.VMEM((layers, rows * level.size, LANES), jnp.float32)


def call(kernel, out_shape, scratch_shapes=(), limit=48):
    return pl.pallas_call(
        kernel,
        out_shape=out_shape,
        scratch_shapes=list(scratch_shapes),
        compiler_params=pltpu.CompilerParams(vmem_limit_bytes=limit * 1024 * 1024),
    )


def shards(stream_now, vorticity):
    _, rows, columns = stream_now.shape
    count = lax.axis_size("wide")
    tiles = columns // (SUBS * LANES)
    fine, mid = Level(0, tiles, 1), Level(1, tiles // 2, 1)
    two, three, four = Level(2, tiles // 4, 1), Level(3, tiles // 4, 2), Level(4, tiles // 4, 4)
    core_swap = [(i, i ^ 1) for i in range(count)]
    chip_swap = [(i, ((i + 1) ^ 1) - 1) for i in range(1, count - 1)]
    chip_swap += [(0, count - 1), (count - 1, 0)]

    def exchange(near, far):
        return lax.ppermute(near, "wide", core_swap), lax.ppermute(far, "wide", chip_swap)

    x, near, far = call(
        functools.partial(pack_kernel, fine, rows),
        [shape(4, rows * fine.size, LANES)] + [shape(4, HALO * fine.size, LANES)] * 2,
    )(stream_now, vorticity)
    near, far = exchange(near, far)
    half = rows // 2
    total = rows + 2 * HALO
    vorticity_next, b0, v0, b1, near, far = call(
        functools.partial(fine_kernel, fine, mid, rows),
        [
            shape(2, rows, columns),
            shape(2, (rows + 2) * fine.size, LANES),
            shape(2, (rows + 4) * fine.size, LANES),
            shape(2, half * mid.size, LANES),
            shape(2, HALO * mid.size, LANES),
            shape(2, HALO * mid.size, LANES),
        ],
        [scratch(4, total, fine)] * 3 + [scratch(2, total, fine)] * 2,
    )(x, near, far)
    near, far = exchange(near, far)
    quarter = rows // 4
    chips = count // 2
    b1, v1, b2 = call(
        functools.partial(middle_kernel, mid, two, half),
        [
            shape(2, (half + 2 * HALO) * mid.size, LANES),
            shape(2, (half + 2 * HALO) * mid.size, LANES),
            shape(chips, 2, quarter * two.size, LANES),
        ],
        [scratch(2, half + 2 * HALO, mid), scratch(2, quarter, two)],
    )(b1, near, far)
    groups = [[i for i in range(count) if i % 2 == c] for c in range(2)]
    same = lax.all_to_all(b2, "wide", 0, 0, axis_index_groups=groups)
    other = lax.ppermute(same, "wide", core_swap)
    n2, n3, n4 = count * quarter, count * quarter // 2, count * quarter // 4
    stream_next = call(
        functools.partial(coarse_kernel, (fine, mid, two, three, four), rows),
        shape(2, rows, columns),
        [scratch(2, n2 + 2 * PAD, two)] * 3
        + [scratch(2, n3 + 2 * PAD, three)] * 3
        + [scratch(2, n4, four)]
        + [scratch(2, n4 + 2 * PAD, four)] * 2
        + [scratch(2, half + 2 * HALO, mid)] * 2
        + [scratch(2, rows + 4, fine)] * 2,
    )(same, other, b1, v1, b0, v0)
    return (vorticity_next, stream_next)


def solution(mesh):
    return jax.shard_map(
        shards,
        mesh=mesh,
        in_specs=(P("member", "wide", None), P("member", "wide", None)),
        out_specs=(P("member", "wide", None), P("member", "wide", None)),
        check_vma=False,
    )
```

time: 313 us -> 54.1 us (0.17)
  the two profiles are of different devices: /device:TPU:8 before, /device:TPU:0 now
where the time goes in v1:
time: 54.1 us; the launch traced here: 53.8 us
  Pallas kernels  19.9 us (37%)
  starting transfers between devices  12.2 us (23%)
  blocking collectives  11.8 us (22%)
  waiting for transfers between devices  7.23 us (13%)
  local copies, waits for them, and re-layouts  2.08 us (4%)
  between operations  0.66 us (1%)
    all_to_all x1, blocking collectives, shards(): same = lax.all_to_all(b2, 'wide', 0, 0, axis_index_groups=groups)  11.8 us
    ppermute x2, starting transfers between devices, exchange(): lax.ppermute(far, 'wide', chip_swap)  10.1 us
    pallas_call x1, Pallas kernels, shards(): call(functools.partial(coarse_kernel, (fine, mid, two, three, four), rows...  9.84 us
    pallas_call x1, Pallas kernels, shards(): call(functools.partial(fine_kernel, fine, mid, rows), [shape(2, rows, col...  8.12 us
    ppermute x2, waiting for transfers between devices, exchange(): lax.ppermute(far, 'wide', chip_swap)  6.06 us
    unnamed x4, local copies, waits for them, and re-layouts  2.08 us
    ppermute x1, starting transfers between devices, shards(): other = lax.ppermute(same, 'wide', core_swap)  1.58 us
    pallas_call x1, Pallas kernels, shards(): call(functools.partial(middle_kernel, mid, two, half), [shape(2, (half +...  1.24 us
  transfers between devices with their start and end apart: 5, of which 3 were waited for; matrix products, arithmetic and copies ran while one was open for 0% of the time, Pallas kernels for 0%

profile of v1, /device:TPU:0, one launch (start us, length us, event | category | flops | bytes accessed | tf_op | source)
XLA Modules:
  0.0 53.8 jit_solution(10655599657107477120)
XLA Ops:
  0.6 0.0 copy-start
  0.6 1.0 %copy-done = f32[2,16,4096]{2,1,0:T(8,128)S(1)} copy-done((f32[2,16,4096]{2,1,0:T(8,128)S(1)}, f32[2,16,4096]{2,1,0:T(8,128)}, u32[]{:S(2)}) %copy-start) | copy-done | bytes 524312
  1.7 0.0 copy-start.1
  1.7 1.0 %copy-done.1 = f32[2,16,4096]{2,1,0:T(8,128)S(1)} copy-done((f32[2,16,4096]{2,1,0:T(8,128)S(1)}, f32[2,16,4096]{2,1,0:T(8,128)}, u32[]{:S(2)}) %copy-start.1) | copy-done | bytes 524312
  2.7 0.7 %shard_map.41 = (f32[4,512,128]{2,1,0:T(8,128)S(1)}, f32[4,128,128]{2,1,0:T(8,128)S(1)}, f32[4,128,128]{2,1,0:T(8,128)S(1)}) custom-call(f32[2,16,4096]{2,1,0:T(8,128)S(1)} %copy-done, f32[2,16,4096]{2,1,0:T(8,128)S(1)} %copy-done.1), custom_call_target="tpu_custom_call" | custom-call | tf_op jit(solution)/shard_map/pallas_call | solution.py:514
  3.4 0.6 %collective-permute-start = (f32[4,128,128]{2,1,0:T(8,128)S(1)}, f32[4,128,128]{2,1,0:T(8,128)S(1)}, u32[]{:S(2)}, u32[]{:S(2)}) collective-permute-start(f32[4,128,128]{2,1,0:T(8,128)S(1)} %get-tuple-element.15), channel_id=1, source_target_pairs={{0,1},{1,0},{2,3},{3,2},{4,5},{5,4},{6,7},{7,6},{8,9},{9,8},{10,11... | collective-permute-start | bytes 786440 | tf_op jit(solution)/shard_map/ppermute | solution.py:512
  4.0 5.7 %collective-permute-start.1 = (f32[4,128,128]{2,1,0:T(8,128)S(1)}, f32[4,128,128]{2,1,0:T(8,128)S(1)}, u32[]{:S(2)}, u32[]{:S(2)}) collective-permute-start(f32[4,128,128]{2,1,0:T(8,128)S(1)} %get-tuple-element.16), channel_id=1, source_target_pairs={{1,2},{2,1},{3,4},{4,3},{5,6},{6,5},{7,8},{8,7},{9,10},{10,9},{11,... | collective-permute-start | bytes 786440 | tf_op jit(solution)/shard_map/ppermute | solution.py:512
  9.6 0.0 collective-permute-done.near_ref
  9.6 4.1 %collective-permute-done.1.far_ref = f32[4,128,128]{2,1,0:T(8,128)S(1)} collective-permute-done((f32[4,128,128]{2,1,0:T(8,128)S(1)}, f32[4,128,128]{2,1,0:T(8,128)S(1)}, u32[]{:S(2)}, u32[]{:S(2)}) %collective-permute-start.1) | collective-permute-done | bytes 262176 | tf_op jit(solution)/shard_map/ppermute | solution.py:512
  13.7 8.1 %shard_map.42 = (f32[2,16,4096]{2,1,0:T(8,128)}, f32[2,576,128]{2,1,0:T(8,128)S(1)}, f32[2,640,128]{2,1,0:T(8,128)S(1)}, f32[2,128,128]{2,1,0:T(8,128)S(1)}, f32...) custom-call(f32[4,512,128]{2,1,0:T(8,128)S(1)} %get-tuple-element.14.x_ref, ...), custom_call_target="tpu_custom_call" | custom-call | tf_op jit(solution)/shard_map/pallas_call | solution.py:521
  21.8 0.0 collective-permute-start.2
  21.8 4.4 %collective-permute-start.3 = (f32[2,64,128]{2,1,0:T(8,128)S(1)}, f32[2,64,128]{2,1,0:T(8,128)S(1)}, u32[]{:S(2)}, u32[]{:S(2)}) collective-permute-start(f32[2,64,128]{2,1,0:T(8,128)S(1)} %get-tuple-element.20), channel_id=1, source_target_pairs={{1,2},{2,1},{3,4},{4,3},{5,6},{6,5},{7,8},{8,7},{9,10},{10,9},{11,... | collective-permute-start | bytes 196616 | tf_op jit(solution)/shard_map/ppermute | solution.py:512
  26.2 0.0 collective-permute-done.2.near_ref
  26.2 2.0 %collective-permute-done.3.far_ref = f32[2,64,128]{2,1,0:T(8,128)S(1)} collective-permute-done((f32[2,64,128]{2,1,0:T(8,128)S(1)}, f32[2,64,128]{2,1,0:T(8,128)S(1)}, u32[]{:S(2)}, u32[]{:S(2)}) %collective-permute-start.3) | collective-permute-done | bytes 65568 | tf_op jit(solution)/shard_map/ppermute | solution.py:512
  28.2 1.2 %shard_map.43 = (f32[2,256,128]{2,1,0:T(8,128)S(1)}, f32[2,256,128]{2,1,0:T(8,128)S(1)}, f32[8,2,32,128]{3,2,1,0:T(8,128)S(1)}) custom-call(f32[2,128,128]{2,1,0:T(8,128)S(1)} %get-tuple-element.18.b_own, f32[2,64,128]{2,1,0:T(8,128)S(1)} %collective-permute-done.2.near_ref, f32[2,64,128]{2,1,0:T(8,128)S(1)} %collective-permute-done.3.far_ref), custom_call_target="tpu_custom_call" | custom-call | tf_op jit(solution)/shard_map/pallas_call | solution.py:536
  29.5 11.8 %all_to_all.5.same_ref = f32[8,2,32,128]{3,2,1,0:T(8,128)S(1)} all-to-all(f32[8,2,32,128]{3,2,1,0:T(8,128)S(1)} %get-tuple-element.21), channel_id=1, replica_groups={{0,2,4,6,8,10,12,14},{1,3,5,7,9,11,13,15},{16,18,20,22,24,26,28,30},{17..., dimensions={0} | all-to-all | bytes 524288 | tf_op jit(solution)/shard_map/all_to_all | solution.py:546
  41.3 1.6 %collective-permute-start.4 = (f32[8,2,32,128]{3,2,1,0:T(8,128)S(1)}, f32[8,2,32,128]{3,2,1,0:T(8,128)S(1)}, u32[]{:S(2)}, u32[]{:S(2)}) collective-permute-start(f32[8,2,32,128]{3,2,1,0:T(8,128)S(1)} %all_to_all.5.same_ref), channel_id=1, source_target_pairs={{0,1},{1,0},{2,3},{3,2},{4,5},{5,4},{6,7},{7,6},{8,9},{9,8},{10,11... | collective-permute-start | bytes 786440 | tf_op jit(solution)/shard_map/ppermute | solution.py:547
  42.8 1.2 %collective-permute-done.4.other_ref = f32[8,2,32,128]{3,2,1,0:T(8,128)S(1)} collective-permute-done((f32[8,2,32,128]{3,2,1,0:T(8,128)S(1)}, f32[8,2,32,128]{3,2,1,0:T(8,128)S(1)}, u32[]{:S(2)}, u32[]{:S(2)}) %collective-permute-start.4) | collective-permute-done | bytes 262176 | tf_op jit(solution)/shard_map/ppermute | solution.py:547
  44.0 9.8 %shard_map.44 = f32[2,16,4096]{2,1,0:T(8,128)} custom-call(f32[8,2,32,128]{3,2,1,0:T(8,128)S(1)} %all_to_all.5.same_ref, f32[8,2,32,128]{3,2,1,0:T(8,128)S(1)} %collective-permute-done.4.other_ref, f32[2,256,128]{2,1,0:T(8,128)S(1)} %get-tuple-element.22.b1_ref, f32[2,256,128]{2,1,0:T(8,128)S(1)} %get-tuple-element.23.v1_ref, ...), custom_call_target="tpu_custom_call" | custom-call | tf_op jit(solution)/shard_map/pallas_call | solution.py:549
Async XLA Ops:
  0.6 1.0 %copy-start = (f32[2,16,4096]{2,1,0:T(8,128)S(1)}, f32[2,16,4096]{2,1,0:T(8,128)}, u32[]{:S(2)}) copy-start(f32[2,16,4096]{2,1,0:T(8,128)} %p_ref.1) | copy-start | bytes 1572868
  1.7 1.0 %copy-start.1 = (f32[2,16,4096]{2,1,0:T(8,128)S(1)}, f32[2,16,4096]{2,1,0:T(8,128)}, u32[]{:S(2)}) copy-start(f32[2,16,4096]{2,1,0:T(8,128)} %q_ref.1) | copy-start | bytes 1572868
  3.4 6.2 %collective-permute-start = (f32[4,128,128]{2,1,0:T(8,128)S(1)}, f32[4,128,128]{2,1,0:T(8,128)S(1)}, u32[]{:S(2)}, u32[]{:S(2)}) collective-permute-start(f32[4,128,128]{2,1,0:T(8,128)S(1)} %get-tuple-element.15), channel_id=1, source_target_pairs={{0,1},{1,0},{2,3},{3,2},{4,5},{5,4},{6,7},{7,6},{8,9},{9,8},{10,11... | collective-permute-start | bytes 786440 | tf_op jit(solution)/shard_map/ppermute | solution.py:512
  4.0 9.7 %collective-permute-start.1 = (f32[4,128,128]{2,1,0:T(8,128)S(1)}, f32[4,128,128]{2,1,0:T(8,128)S(1)}, u32[]{:S(2)}, u32[]{:S(2)}) collective-permute-start(f32[4,128,128]{2,1,0:T(8,128)S(1)} %get-tuple-element.16), channel_id=1, source_target_pairs={{1,2},{2,1},{3,4},{4,3},{5,6},{6,5},{7,8},{8,7},{9,10},{10,9},{11,... | collective-permute-start | bytes 786440 | tf_op jit(solution)/shard_map/ppermute | solution.py:512
  21.8 4.4 %collective-permute-start.2 = (f32[2,64,128]{2,1,0:T(8,128)S(1)}, f32[2,64,128]{2,1,0:T(8,128)S(1)}, u32[]{:S(2)}, u32[]{:S(2)}) collective-permute-start(f32[2,64,128]{2,1,0:T(8,128)S(1)} %get-tuple-element.19), channel_id=1, source_target_pairs={{0,1},{1,0},{2,3},{3,2},{4,5},{5,4},{6,7},{7,6},{8,9},{9,8},{10,11... | collective-permute-start | bytes 196616 | tf_op jit(solution)/shard_map/ppermute | solution.py:512
  21.8 6.4 %collective-permute-start.3 = (f32[2,64,128]{2,1,0:T(8,128)S(1)}, f32[2,64,128]{2,1,0:T(8,128)S(1)}, u32[]{:S(2)}, u32[]{:S(2)}) collective-permute-start(f32[2,64,128]{2,1,0:T(8,128)S(1)} %get-tuple-element.20), channel_id=1, source_target_pairs={{1,2},{2,1},{3,4},{4,3},{5,6},{6,5},{7,8},{8,7},{9,10},{10,9},{11,... | collective-permute-start | bytes 196616 | tf_op jit(solution)/shard_map/ppermute | solution.py:512
  41.3 2.7 %collective-permute-start.4 = (f32[8,2,32,128]{3,2,1,0:T(8,128)S(1)}, f32[8,2,32,128]{3,2,1,0:T(8,128)S(1)}, u32[]{:S(2)}, u32[]{:S(2)}) collective-permute-start(f32[8,2,32,128]{3,2,1,0:T(8,128)S(1)} %all_to_all.5.same_ref), channel_id=1, source_target_pairs={{0,1},{1,0},{2,3},{3,2},{4,5},{5,4},{6,7},{7,6},{8,9},{9,8},{10,11... | collective-permute-start | bytes 786440 | tf_op jit(solution)/shard_map/ppermute | solution.py:547

commit v2 on v1

--- a/solution.py
+++ b/solution.py
@@ -10,7 +10,8 @@
 
 LANES = 128
 SUBS = 8
-HALO = 4
+HALO = 3
+MID_HALO = 4
 RELAX = 0.8
 COUPLING = (0.02, 0.04)
 TIME_STEP = 0.5
@@ -235,74 +236,64 @@
     return me, lax.rem(me, 2), me == 0, me == count - 1
 
 
-def to_native(dst, src, level, src_at, rows):
-    for layer in range(2):
+def pack_kernel(level, rows, p_ref, q_ref, ext_ref, near_ref, far_ref, native, sems):
+    copies = []
+    for field, ref in enumerate((p_ref, q_ref)):
+        for layer in range(2):
+            which = 2 * field + layer
+            copies.append(
+                pltpu.make_async_copy(ref.at[layer], native.at[which], sems.at[which])
+            )
+            copies[-1].start()
+    for which in range(4):
+        copies[which].wait()
         for group in range(rows // SUBS):
             for t in range(level.tiles):
                 for s in range(SUBS):
-                    first = (src_at + group * SUBS) * level.size + t * SUBS + s
+                    first = (HALO + group * SUBS) * level.size + t * SUBS + s
                     column = (s * level.tiles + t) * LANES
-                    dst[layer, group * SUBS : (group + 1) * SUBS, column : column + LANES] = src[
-                        layer, pl.ds(first, SUBS, stride=level.size), :
+                    ext_ref[which, pl.ds(first, SUBS, stride=level.size), :] = native[
+                        which, group * SUBS : (group + 1) * SUBS, column : column + LANES
                     ]
-
-
-def pack_kernel(level, rows, p_ref, q_ref, x_ref, near_ref, far_ref):
-    for field, ref in enumerate((p_ref, q_ref)):
-        for layer in range(2):
-            for group in range(rows // SUBS):
-                for t in range(level.tiles):
-                    for s in range(SUBS):
-                        first = group * SUBS * level.size + t * SUBS + s
-                        column = (s * level.tiles + t) * LANES
-                        x_ref[2 * field + layer, pl.ds(first, SUBS, stride=level.size), :] = ref[
-                            layer, group * SUBS : (group + 1) * SUBS, column : column + LANES
-                        ]
-    send_edges(level, rows, x_ref, 0, near_ref, far_ref)
-
-
-def send_edges(level, rows, src, src_at, near_ref, far_ref):
+    send_edges(level, HALO, HALO, rows, ext_ref, near_ref, far_ref)
+
+
+def send_edges(level, width, src_at, rows, src, near_ref, far_ref):
     _, odd, _, _ = place()
-    size = HALO * level.size
-    last = (src_at + rows - HALO) * level.size
+    size = width * level.size
+    last = (src_at + rows - width) * level.size
     top = src_at * level.size
     near = pl.multiple_of(jnp.where(odd == 1, top, last), SUBS)
     far = pl.multiple_of(jnp.where(odd == 1, last, top), SUBS)
-    near_ref[...] = src[:, pl.ds(near, size), :]
-    far_ref[...] = src[:, pl.ds(far, size), :]
-
-
-def join(level, rows, dst, own, near_ref, far_ref):
+    near_ref[:, 0:size, :] = src[:, pl.ds(near, size), :]
+    far_ref[:, 0:size, :] = src[:, pl.ds(far, size), :]
+
+
+def receive_edges(level, width, dst_at, rows, dst, near_ref, far_ref):
     _, odd, first, last = place()
-    size = HALO * level.size
-    low = (HALO + rows) * level.size
-    near = pl.multiple_of(jnp.where(odd == 1, 0, low), SUBS)
-    far = pl.multiple_of(jnp.where(odd == 1, low, 0), SUBS)
-    dst[:, size : size + rows * level.size, :] = own[...]
-    dst[:, pl.ds(near, size), :] = near_ref[...]
+    size = width * level.size
+    low = (dst_at + rows) * level.size
+    top = (dst_at - width) * level.size
+    near = pl.multiple_of(jnp.where(odd == 1, top, low), SUBS)
+    far = pl.multiple_of(jnp.where(odd == 1, low, top), SUBS)
+    dst[:, pl.ds(near, size), :] = near_ref[:, 0:size, :]
     outside = jnp.logical_or(first, last)
-    dst[:, pl.ds(far, size), :] = jnp.where(outside, 0.0, far_ref[...])
-
-
-def fine_kernel(
-    level, coarse, rows, x_ref, near_ref, far_ref,
-    next_ref, b_ref, v_ref, bc_ref, bc_near_ref, bc_far_ref,
-    ext, e_ref, w_ref, b_all, v_one,
-):
-    _, _, is_first, is_last = place()
-    total = rows + 2 * HALO
-    join(level, rows, ext, x_ref, near_ref, far_ref)
-
-    def shift_body(first, count):
+    dst[:, pl.ds(far, size), :] = jnp.where(outside, 0.0, far_ref[:, 0:size, :])
+
+
+def shift_rows(level, ext, e_ref, w_ref, low, high, block):
+    def body(first, count):
         for k in range(count):
             for f in range(4):
                 v = load(ext, level, f, first + k)
                 store(e_ref, level, f, first + k, east(v))
                 store(w_ref, level, f, first + k, west(v))
 
-    row_blocks(0, total, 2, shift_body)
-
-    def advance_body(first, count):
+    row_blocks(low, high, block, body)
+
+
+def advance_rows(level, b_ref, ext, e_ref, w_ref, low, high, block):
+    def body(first, count):
         for layer in range(2):
             for t in range(level.tiles):
                 def grab(ref, field):
@@ -325,73 +316,117 @@
                     if layer == 1:
                         lap = (p[n] + p[s]) + (pe[k] + pw[k]) - 4.0 * p[k]
                         step = step + (TIME_STEP * DRAG[1]) * lap
-                    b_all[layer, at(level, first + k, t), :] = step - q[k]
-
-    row_blocks(1, total - 1, 2, advance_body)
-
-    sweep(level, v_one, 0, ext, 0, b_all, 0, 1, total - 1, 2)
-
-    @pl.when(is_first)
-    def _():
-        clear(v_one, level, 0, HALO)
-
-    @pl.when(is_last)
-    def _():
-        clear(v_one, level, HALO + rows, total)
-
-    sweep(level, v_ref, -2, v_one, 0, b_all, 0, 2, total - 2, 2)
-
-    @pl.when(is_first)
-    def _():
-        clear(v_ref, level, 0, 2)
-
-    @pl.when(is_last)
-    def _():
-        clear(v_ref, level, rows + 2, rows + 4)
-
-    restrict(level, bc_ref, 0, coarse, v_ref, 2, b_all, HALO, 0, rows // 2, 1)
-    send_edges(coarse, rows // 2, bc_ref, 0, bc_near_ref, bc_far_ref)
-    b_ref[...] = b_all[:, 3 * level.size : (total - 3) * level.size, :]
+                    b_ref[layer, at(level, first + k, t), :] = step - q[k]
+
+    row_blocks(low, high, block, body)
+
+
+def inner_kernel(level, coarse, rows, ext, e_ref, w_ref, b_ref, v_one, v_two, bc_ref):
+    low, high = HALO, HALO + rows
+    shift_rows(level, ext, e_ref, w_ref, low, high, 4)
+    advance_rows(level, b_ref, ext, e_ref, w_ref, low + 1, high - 1, 2)
+    sweep(level, v_one, 0, ext, 0, b_ref, 0, low + 2, high - 2, 4)
+    sweep(level, v_two, 0, v_one, 0, b_ref, 0, low + 3, high - 3, 4)
+    restrict(level, bc_ref, 0, coarse, v_two, HALO, b_ref, HALO, 2, rows // 2 - 2, 2)
+
+
+def outer_kernel(level, coarse, rows, *refs):
+    near_ref, far_ref = refs[7:9]
+    ext, e_ref, w_ref, b_ref, v_one, v_two, bc_ref, bc_near_ref, bc_far_ref = refs[9:]
+    _, _, is_first, is_last = place()
+    low, high = HALO, HALO + rows
+    total = rows + 2 * HALO
+    receive_edges(level, HALO, HALO, rows, ext, near_ref, far_ref)
+    shift_rows(level, ext, e_ref, w_ref, 0, low, 3)
+    shift_rows(level, ext, e_ref, w_ref, high, total, 3)
+    advance_rows(level, b_ref, ext, e_ref, w_ref, 1, low + 1, 3)
+    advance_rows(level, b_ref, ext, e_ref, w_ref, high - 1, total - 1, 3)
+    sweep(level, v_one, 0, ext, 0, b_ref, 0, 1, low + 2, 4)
+    sweep(level, v_one, 0, ext, 0, b_ref, 0, high - 2, total - 1, 4)
+
+    def trim(ref):
+        @pl.when(is_first)
+        def _():
+            clear(ref, level, 0, HALO)
+
+        @pl.when(is_last)
+        def _():
+            clear(ref, level, high, total)
+
+    trim(v_one)
+    sweep(level, v_two, 0, v_one, 0, b_ref, 0, 2, low + 3, 4)
+    sweep(level, v_two, 0, v_one, 0, b_ref, 0, high - 3, total - 2, 4)
+    trim(v_two)
+    half = rows // 2
+    restrict(level, bc_ref, 0, coarse, v_two, HALO, b_ref, HALO, 0, 2, 2)
+    restrict(level, bc_ref, 0, coarse, v_two, HALO, b_ref, HALO, half - 2, half, 2)
+    send_edges(coarse, MID_HALO, 0, half, bc_ref, bc_near_ref, bc_far_ref)
+    _, odd, _, _ = place()
+    first = MID_HALO * coarse.size
+    top, last = (low + 1) * level.size, (high - 2) * level.size
+    near = pl.multiple_of(jnp.where(odd == 1, top, last), SUBS)
+    far = pl.multiple_of(jnp.where(odd == 1, last, top), SUBS)
+    bc_near_ref[:, first : first + level.size, :] = v_two[:, pl.ds(near, level.size), :]
+    bc_far_ref[:, first : first + level.size, :] = v_two[:, pl.ds(far, level.size), :]
+
+
+def emit_kernel(level, rows, b_ref, next_ref, native, sems):
+    copies = []
     for layer in range(2):
         for group in range(rows // SUBS):
+            rows_of = pl.ds(group * SUBS, SUBS)
             for t in range(level.tiles):
                 for s in range(SUBS):
                     first = (HALO + group * SUBS) * level.size + t * SUBS + s
                     column = (s * level.tiles + t) * LANES
-                    next_ref[
-                        layer, group * SUBS : (group + 1) * SUBS, column : column + LANES
-                    ] = -b_all[layer, pl.ds(first, SUBS, stride=level.size), :]
+                    native[layer, rows_of, column : column + LANES] = -b_ref[
+                        layer, pl.ds(first, SUBS, stride=level.size), :
+                    ]
+            copies.append(
+                pltpu.make_async_copy(
+                    native.at[layer, rows_of], next_ref.at[layer, rows_of],
+                    sems.at[layer, group],
+                )
+            )
+            copies[-1].start()
+    for copy in copies:
+        copy.wait()
 
 
 def middle_kernel(
-    level, coarse, rows, b_own, near_ref, far_ref, b_ref, v_ref, out_ref, v_one, bc
+    fine, level, coarse, rows, b_own, near_ref, far_ref, v0_in,
+    b_ref, v_ref, out_ref, v0_ref, v_one, bc,
 ):
-    _, _, is_first, is_last = place()
-    total = rows + 2 * HALO
-    join(level, rows, b_ref, b_own, near_ref, far_ref)
+    _, odd, is_first, is_last = place()
+    total = rows + 2 * MID_HALO
+    edge = MID_HALO * level.size
+    b_ref[:, edge : edge + rows * level.size, :] = b_own[...]
+    receive_edges(level, MID_HALO, MID_HALO, rows, b_ref, near_ref, far_ref)
     start(level, v_one, 0, b_ref, 0, 0, total, 4)
 
-    @pl.when(is_first)
-    def _():
-        clear(v_one, level, 0, HALO)
-
-    @pl.when(is_last)
-    def _():
-        clear(v_one, level, HALO + rows, total)
-
-    sweep(level, v_ref, 0, v_one, 0, b_ref, 0, 1, total - 1, 2)
-
-    @pl.when(is_first)
-    def _():
-        clear(v_ref, level, 0, HALO)
-
-    @pl.when(is_last)
-    def _():
-        clear(v_ref, level, HALO + rows, total)
-
-    restrict(level, bc, 0, coarse, v_ref, HALO, b_ref, HALO, 0, rows // 2, 2)
+    def trim(ref):
+        @pl.when(is_first)
+        def _():
+            clear(ref, level, 0, MID_HALO)
+
+        @pl.when(is_last)
+        def _():
+            clear(ref, level, MID_HALO + rows, total)
+
+    trim(v_one)
+    sweep(level, v_ref, 0, v_one, 0, b_ref, 0, 1, total - 1, 7)
+    trim(v_ref)
+    restrict(level, bc, 0, coarse, v_ref, MID_HALO, b_ref, MID_HALO, 0, rows // 2, 4)
     for copy in range(out_ref.shape[0]):
         out_ref[copy] = bc[...]
+    top, low = (HALO - 2) * fine.size, (HALO + 2 * rows + 1) * fine.size
+    near = pl.multiple_of(jnp.where(odd == 1, top, low), SUBS)
+    far = pl.multiple_of(jnp.where(odd == 1, low, top), SUBS)
+    v0_ref[:, pl.ds(near, fine.size), :] = near_ref[:, edge : edge + fine.size, :]
+    outside = jnp.logical_or(is_first, is_last)
+    v0_ref[:, pl.ds(far, fine.size), :] = jnp.where(
+        outside, 0.0, far_ref[:, edge : edge + fine.size, :]
+    )
 
 
 PAD = 4
@@ -399,7 +434,7 @@
 
 def coarse_kernel(
     levels, rows, same_ref, other_ref, b1_ref, v1_ref, b0_ref, v0_ref, out_ref,
-    b2, v2, w2, b3, v3, w3, b4, v4, w4, x1, y1, x0, y0,
+    b2, v2, w2, b3, v3, w3, b4, v4, w4, x1, y1, x0, y0, native, sems,
 ):
     me, odd, is_first, is_last = place()
     fine, mid, two, three, four = levels
@@ -455,7 +490,7 @@
     trim(v2, two, n2)
 
     n1 = rows // 2
-    total = n1 + 2 * HALO
+    total = n1 + 2 * MID_HALO
 
     def trim_own(ref, level, halo, n):
         @pl.when(is_first)
@@ -467,18 +502,39 @@
             clear(ref, level, halo + n, 2 * halo + n)
 
     correct(
-        mid, two, x1, 0, v1_ref, 0, v2, PAD + me * own - HALO // 2, 0, total // 2, 2
+        mid, two, x1, 0, v1_ref, 0, v2, PAD + me * own - MID_HALO // 2, 0, total // 2, 4
     )
-    sweep(mid, y1, 0, x1, 0, b1_ref, 0, 2, total - 2, 2)
-    trim_own(y1, mid, HALO, n1)
-    sweep(mid, x1, 0, y1, 0, b1_ref, 0, 3, total - 3, 2)
-    trim_own(x1, mid, HALO, n1)
-
-    correct(fine, mid, x0, 0, v0_ref, 0, x1, HALO - 1, 0, n1 + 2, 1)
-    sweep(fine, y0, 0, x0, 0, b0_ref, -1, 1, rows + 3, 2)
-    trim_own(y0, fine, 2, rows)
-    sweep(fine, x0, 0, y0, 0, b0_ref, -1, 2, rows + 2, 2)
-    to_native(out_ref, x0, fine, 2, rows)
+    sweep(mid, y1, 0, x1, 0, b1_ref, 0, 2, total - 2, 6)
+    trim_own(y1, mid, MID_HALO, n1)
+    sweep(mid, x1, 0, y1, 0, b1_ref, 0, 3, total - 3, 5)
+    trim_own(x1, mid, MID_HALO, n1)
+
+    low, high = HALO, HALO + rows
+    correct(fine, mid, x0, HALO - 2, v0_ref, HALO - 2, x1, MID_HALO - 1, 0, n1 + 2, 2)
+    sweep(fine, y0, 0, x0, 0, b0_ref, 0, low - 1, high + 1, 4)
+    trim_own(y0, fine, HALO, rows)
+    copies = []
+    for group in range(rows // SUBS):
+        first_row = low + group * SUBS
+        rows_of = pl.ds(group * SUBS, SUBS)
+        sweep(fine, x0, 0, y0, 0, b0_ref, 0, first_row, first_row + SUBS, 4)
+        for layer in range(2):
+            for t in range(fine.tiles):
+                for s in range(SUBS):
+                    first = first_row * fine.size + t * SUBS + s
+                    column = (s * fine.tiles + t) * LANES
+                    native[layer, rows_of, column : column + LANES] = x0[
+                        layer, pl.ds(first, SUBS, stride=fine.size), :
+                    ]
+            copies.append(
+                pltpu.make_async_copy(
+                    native.at[layer, rows_of], out_ref.at[layer, rows_of],
+                    sems.at[layer, group],
+                )
+            )
+            copies[-1].start()
+    for copy in copies:
+        copy.wait()
 
 
 def shape(*dims):
@@ -489,12 +545,20 @@
     return pltpu.VMEM((layers, rows * level.size, LANES), jnp.float32)
 
 
-def call(kernel, out_shape, scratch_shapes=(), limit=48):
+HBM = pl.BlockSpec(memory_space=pltpu.HBM)
+VMEM = pl.BlockSpec(memory_space=pltpu.VMEM)
+
+
+def call(kernel, out_shape, scratch_shapes=(), cost=None, limit=24, **options):
+    if cost is not None:
+        cost = pl.CostEstimate(flops=cost, bytes_accessed=cost // 8, transcendentals=0)
     return pl.pallas_call(
         kernel,
         out_shape=out_shape,
         scratch_shapes=list(scratch_shapes),
+        cost_estimate=cost,
         compiler_params=pltpu.CompilerParams(vmem_limit_bytes=limit * 1024 * 1024),
+        **options,
     )
 
 
@@ -507,43 +571,62 @@
     core_swap = [(i, i ^ 1) for i in range(count)]
     chip_swap = [(i, ((i + 1) ^ 1) - 1) for i in range(1, count - 1)]
     chip_swap += [(0, count - 1), (count - 1, 0)]
+    groups = rows // SUBS
 
     def exchange(near, far):
         return lax.ppermute(near, "wide", core_swap), lax.ppermute(far, "wide", chip_swap)
 
-    x, near, far = call(
+    half, quarter = rows // 2, rows // 4
+    total = rows + 2 * HALO
+    ext, near, far = call(
         functools.partial(pack_kernel, fine, rows),
-        [shape(4, rows * fine.size, LANES)] + [shape(4, HALO * fine.size, LANES)] * 2,
+        [shape(4, total * fine.size, LANES)] + [shape(4, HALO * fine.size, LANES)] * 2,
+        [pltpu.VMEM((4, rows, columns), jnp.float32), pltpu.SemaphoreType.DMA((4,))],
+        in_specs=[HBM, HBM],
     )(stream_now, vorticity)
     near, far = exchange(near, far)
-    half = rows // 2
-    total = rows + 2 * HALO
-    vorticity_next, b0, v0, b1, near, far = call(
-        functools.partial(fine_kernel, fine, mid, rows),
+    state = [
+        shape(4, total * fine.size, LANES),
+        shape(4, total * fine.size, LANES),
+        shape(2, total * fine.size, LANES),
+        shape(2, total * fine.size, LANES),
+        shape(2, total * fine.size, LANES),
+        shape(2, half * mid.size, LANES),
+    ]
+    inner = call(
+        functools.partial(inner_kernel, fine, mid, rows),
+        state,
+        cost=8000000,
+    )(ext)
+    edge = shape(2, MID_HALO * mid.size + fine.size, LANES)
+    outer = call(
+        functools.partial(outer_kernel, fine, mid, rows),
+        [shape(4, total * fine.size, LANES)] + state + [edge, edge],
+        input_output_aliases={i: i for i in range(7)},
+    )(ext, *inner, near, far)
+    b0, v0, b1, near, far = outer[3], outer[5], outer[6], outer[7], outer[8]
+    near, far = exchange(near, far)
+    vorticity_next = call(
+        functools.partial(emit_kernel, fine, rows),
+        shape(2, rows, columns),
+        [pltpu.VMEM((2, rows, columns), jnp.float32), pltpu.SemaphoreType.DMA((2, groups))],
+        cost=4000000,
+        out_specs=HBM,
+    )(b0)
+    chips = count // 2
+    b1, v1, b2, v0 = call(
+        functools.partial(middle_kernel, fine, mid, two, half),
         [
-            shape(2, rows, columns),
-            shape(2, (rows + 2) * fine.size, LANES),
-            shape(2, (rows + 4) * fine.size, LANES),
-            shape(2, half * mid.size, LANES),
-            shape(2, HALO * mid.size, LANES),
-            shape(2, HALO * mid.size, LANES),
+            shape(2, (half + 2 * MID_HALO) * mid.size, LANES),
+            shape(2, (half + 2 * MID_HALO) * mid.size, LANES),
+            shape(chips, 2, quarter * two.size, LANES),
+            shape(2, total * fine.size, LANES),
         ],
-        [scratch(4, total, fine)] * 3 + [scratch(2, total, fine)] * 2,
-    )(x, near, far)
-    near, far = exchange(near, far)
-    quarter = rows // 4
-    chips = count // 2
-    b1, v1, b2 = call(
-        functools.partial(middle_kernel, mid, two, half),
-        [
-            shape(2, (half + 2 * HALO) * mid.size, LANES),
-            shape(2, (half + 2 * HALO) * mid.size, LANES),
-            shape(chips, 2, quarter * two.size, LANES),
-        ],
-        [scratch(2, half + 2 * HALO, mid), scratch(2, quarter, two)],
-    )(b1, near, far)
-    groups = [[i for i in range(count) if i % 2 == c] for c in range(2)]
-    same = lax.all_to_all(b2, "wide", 0, 0, axis_index_groups=groups)
+        [scratch(2, half + 2 * MID_HALO, mid), scratch(2, quarter, two)],
+        input_output_aliases={3: 3},
+    )(b1, near, far, v0)
+    cores = [[i for i in range(count) if i % 2 == c] for c in range(2)]
+    same = lax.all_to_all(b2, "wide", 0, 0, axis_index_groups=cores)
     other = lax.ppermute(same, "wide", core_swap)
     n2, n3, n4 = count * quarter, count * quarter // 2, count * quarter // 4
     stream_next = call(
@@ -553,8 +636,11 @@
         + [scratch(2, n3 + 2 * PAD, three)] * 3
         + [scratch(2, n4, four)]
         + [scratch(2, n4 + 2 * PAD, four)] * 2
-        + [scratch(2, half + 2 * HALO, mid)] * 2
-        + [scratch(2, rows + 4, fine)] * 2,
+        + [scratch(2, half + 2 * MID_HALO, mid)] * 2
+        + [scratch(2, total, fine)] * 2
+        + [pltpu.VMEM((2, rows, columns), jnp.float32), pltpu.SemaphoreType.DMA((2, groups))],
+        limit=40,
+        out_specs=HBM,
     )(same, other, b1, v1, b0, v0)
     return (vorticity_next, stream_next)
 

time: 54.1 us -> 44.7 us (0.83)
  Pallas kernels: 19.9 us -> 14.6 us
  waiting for transfers between devices: 7.23 us -> 2.96 us
    pallas_call x3 -> x5, Pallas kernels: 10 us -> 6.52 us  [the longest x1 2.8 us: shards(): call(functools.partial(inner_kernel, fine, mid, rows), state, cost=8000000)]
    ppermute x2, waiting for transfers between devices: 6.06 us -> 2.83 us  [exchange(): lax.ppermute(far, 'wide', chip_swap)]
    pallas_call x1, Pallas kernels: 9.84 us -> 8.11 us  [shards(): call(functools.partial(coarse_kernel, (fine, mid, two, three, four), rows...]
    ppermute x1, waiting for transfers between devices: 1.16 us -> 0.12 us  [shards(): other = lax.ppermute(same, 'wide', core_swap)]
  transfers between devices with their start and end apart: 5 -> 5, of which waited for: 3 -> 3; matrix products, arithmetic and copies ran while one was open for 0% -> 0% of each run, Pallas kernels for 0% -> 9%
where the time goes in v2:
time: 44.7 us; the launch traced here: 44.4 us
  Pallas kernels  14.6 us (33%)
  starting transfers between devices  12.5 us (28%)
  blocking collectives  11.6 us (26%)
  waiting for transfers between devices  2.96 us (7%)
  local copies, waits for them, and re-layouts  2.08 us (5%)
  between operations  0.69 us (2%)
    all_to_all x1, blocking collectives, shards(): same = lax.all_to_all(b2, 'wide', 0, 0, axis_index_groups=cores)  11.6 us
    ppermute x2, starting transfers between devices, exchange(): lax.ppermute(far, 'wide', chip_swap)  10.2 us
    pallas_call x1, Pallas kernels, shards(): call(functools.partial(coarse_kernel, (fine, mid, two, three, four), rows...  8.11 us
    ppermute x2, waiting for transfers between devices, exchange(): lax.ppermute(far, 'wide', chip_swap)  2.83 us
    pallas_call x1, Pallas kernels, shards(): call(functools.partial(inner_kernel, fine, mid, rows), state, cost=8000000)  2.8 us
    unnamed x4, local copies, waits for them, and re-layouts  2.08 us
    ppermute x1, starting transfers between devices, shards(): other = lax.ppermute(same, 'wide', core_swap)  1.7 us
    pallas_call x1, Pallas kernels, shards(): call(functools.partial(outer_kernel, fine, mid, rows), [shape(4, total *...  1.27 us
  transfers between devices with their start and end apart: 5, of which 3 were waited for; matrix products, arithmetic and copies ran while one was open for 0% of the time, Pallas kernels for 9%

profile of v2, /device:TPU:0, one launch (start us, length us, event | category | flops | bytes accessed | tf_op | source)
XLA Modules:
  0.0 44.4 jit_solution(5061579969509267297)
XLA Ops:
  0.6 0.0 copy-start
  0.6 1.0 %copy-done = f32[2,16,4096]{2,1,0:T(8,128)S(1)} copy-done((f32[2,16,4096]{2,1,0:T(8,128)S(1)}, f32[2,16,4096]{2,1,0:T(8,128)}, u32[]{:S(2)}) %copy-start) | copy-done | bytes 524312
  1.7 0.0 copy-start.1
  1.7 1.0 %copy-done.1 = f32[2,16,4096]{2,1,0:T(8,128)S(1)} copy-done((f32[2,16,4096]{2,1,0:T(8,128)S(1)}, f32[2,16,4096]{2,1,0:T(8,128)}, u32[]{:S(2)}) %copy-start.1) | copy-done | bytes 524312
  2.7 0.8 %shard_map.41 = (f32[4,704,128]{2,1,0:T(8,128)S(1)}, f32[4,96,128]{2,1,0:T(8,128)S(1)}, f32[4,96,128]{2,1,0:T(8,128)S(1)}) custom-call(f32[2,16,4096]{2,1,0:T(8,128)S(1)} %copy-done, f32[2,16,4096]{2,1,0:T(8,128)S(1)} %copy-done.1), custom_call_target="tpu_custom_call" | custom-call | tf_op jit(solution)/shard_map/pallas_call | solution.py:581
  3.5 0.6 %collective-permute-start = (f32[4,96,128]{2,1,0:T(8,128)S(1)}, f32[4,96,128]{2,1,0:T(8,128)S(1)}, u32[]{:S(2)}, u32[]{:S(2)}) collective-permute-start(f32[4,96,128]{2,1,0:T(8,128)S(1)} %get-tuple-element.27), channel_id=1, source_target_pairs={{0,1},{1,0},{2,3},{3,2},{4,5},{5,4},{6,7},{7,6},{8,9},{9,8},{10,11... | collective-permute-start | bytes 589832 | tf_op jit(solution)/shard_map/ppermute | solution.py:577
  4.1 5.7 %collective-permute-start.1 = (f32[4,96,128]{2,1,0:T(8,128)S(1)}, f32[4,96,128]{2,1,0:T(8,128)S(1)}, u32[]{:S(2)}, u32[]{:S(2)}) collective-permute-start(f32[4,96,128]{2,1,0:T(8,128)S(1)} %get-tuple-element.28), channel_id=1, source_target_pairs={{1,2},{2,1},{3,4},{4,3},{5,6},{6,5},{7,8},{8,7},{9,10},{10,9},{11,... | collective-permute-start | bytes 589832 | tf_op jit(solution)/shard_map/ppermute | solution.py:577
  9.7 2.8 %shard_map.42 = (f32[4,704,128]{2,1,0:T(8,128)S(1)}, f32[4,704,128]{2,1,0:T(8,128)S(1)}, f32[2,704,128]{2,1,0:T(8,128)S(1)}, f32[2,704,128]{2,1,0:T(8,128)S(1)},...) custom-call(f32[4,704,128]{2,1,0:T(8,128)S(1)} %get-tuple-element.20.ext.refs_0_), custom_call_target="tpu_custom_call" | custom-call | flops 8000000 | bytes 1000000 | tf_op jit(solution)/shard_map/pallas_call | solution.py:596
  12.5 0.0 collective-permute-done.refs_7_
  12.5 0.5 %collective-permute-done.1.refs_8_ = f32[4,96,128]{2,1,0:T(8,128)S(1)} collective-permute-done((f32[4,96,128]{2,1,0:T(8,128)S(1)}, f32[4,96,128]{2,1,0:T(8,128)S(1)}, u32[]{:S(2)}, u32[]{:S(2)}) %collective-permute-start.1) | collective-permute-done | bytes 196640 | tf_op jit(solution)/shard_map/ppermute | solution.py:577
  13.1 1.3 %shard_map.43 = (f32[4,704,128]{2,1,0:T(8,128)S(1)}, f32[4,704,128]{2,1,0:T(8,128)S(1)}, f32[4,704,128]{2,1,0:T(8,128)S(1)}, f32[2,704,128]{2,1,0:T(8,128)S(1)},...) custom-call(f32[4,704,128]{2,1,0:T(8,128)S(1)} %get-tuple-element.20, ...), custom_call_target="tpu_custom_call", output_to_operand_aliasing={{0}: (0, {}), {1}: (1, {}), {2}: (2, {}), {3}: (3, {}), {4}... | custom-call | tf_op jit(solution)/shard_map/pallas_call | solution.py:602
  14.4 0.1 collective-permute-start.2
  14.4 4.5 %collective-permute-start.3 = (f32[2,96,128]{2,1,0:T(8,128)S(1)}, f32[2,96,128]{2,1,0:T(8,128)S(1)}, u32[]{:S(2)}, u32[]{:S(2)}) collective-permute-start(f32[2,96,128]{2,1,0:T(8,128)S(1)} %get-tuple-element.32), channel_id=1, source_target_pairs={{1,2},{2,1},{3,4},{4,3},{5,6},{6,5},{7,8},{8,7},{9,10},{10,9},{11,... | collective-permute-start | bytes 294920 | tf_op jit(solution)/shard_map/ppermute | solution.py:577
  18.9 0.0 collective-permute-done.2.near_ref
  18.9 2.3 %collective-permute-done.3.far_ref = f32[2,96,128]{2,1,0:T(8,128)S(1)} collective-permute-done((f32[2,96,128]{2,1,0:T(8,128)S(1)}, f32[2,96,128]{2,1,0:T(8,128)S(1)}, u32[]{:S(2)}, u32[]{:S(2)}) %collective-permute-start.3) | collective-permute-done | bytes 98336 | tf_op jit(solution)/shard_map/ppermute | solution.py:577
  21.2 0.6 %shard_map.45 = (f32[2,256,128]{2,1,0:T(8,128)S(1)}, f32[2,256,128]{2,1,0:T(8,128)S(1)}, f32[8,2,32,128]{3,2,1,0:T(8,128)S(1)}, f32[2,704,128]{2,1,0:T(8,128)S(1)}) custom-call(f32[2,128,128]{2,1,0:T(8,128)S(1)} %get-tuple-element.30.b_own, f32[2,96,128]{2,1,0:T(8,128)S(1)} %collective-permute-done.2.near_ref, ...), custom_call_target="tpu_custom_call", output_to_operand_aliasing={{3}: (3, {})} | custom-call | tf_op jit(solution)/shard_map/pallas_call | solution.py:617
  21.9 11.6 %all_to_all.5.same_ref = f32[8,2,32,128]{3,2,1,0:T(8,128)S(1)} all-to-all(f32[8,2,32,128]{3,2,1,0:T(8,128)S(1)} %get-tuple-element.34), channel_id=1, replica_groups={{0,2,4,6,8,10,12,14},{1,3,5,7,9,11,13,15},{16,18,20,22,24,26,28,30},{17..., dimensions={0} | all-to-all | bytes 524288 | tf_op jit(solution)/shard_map/all_to_all | solution.py:629
  33.5 1.7 %collective-permute-start.4 = (f32[8,2,32,128]{3,2,1,0:T(8,128)S(1)}, f32[8,2,32,128]{3,2,1,0:T(8,128)S(1)}, u32[]{:S(2)}, u32[]{:S(2)}) collective-permute-start(f32[8,2,32,128]{3,2,1,0:T(8,128)S(1)} %all_to_all.5.same_ref), channel_id=1, source_target_pairs={{0,1},{1,0},{2,3},{3,2},{4,5},{5,4},{6,7},{7,6},{8,9},{9,8},{10,11... | collective-permute-start | bytes 786440 | tf_op jit(solution)/shard_map/ppermute | solution.py:630
  35.2 1.0 %shard_map.44 = f32[2,16,4096]{2,1,0:T(8,128)} custom-call(f32[2,704,128]{2,1,0:T(8,128)S(1)} %get-tuple-element.29.b_ref.b0_ref), custom_call_target="tpu_custom_call" | custom-call | flops 4000000 | bytes 500000 | tf_op jit(solution)/shard_map/pallas_call | solution.py:609
  36.2 0.1 collective-permute-done.4.other_ref
  36.3 8.1 %shard_map.46 = f32[2,16,4096]{2,1,0:T(8,128)} custom-call(f32[8,2,32,128]{3,2,1,0:T(8,128)S(1)} %all_to_all.5.same_ref, f32[8,2,32,128]{3,2,1,0:T(8,128)S(1)} %collective-permute-done.4.other_ref, f32[2,256,128]{2,1,0:T(8,128)S(1)} %get-tuple-element.35.b1_ref, f32[2,256,128]{2,1,0:T(8,128)S(1)} %get-tuple-element.36.v1_ref, ...), custom_call_target="tpu_custom_call" | custom-call | tf_op jit(solution)/shard_map/pallas_call | solution.py:632
Async XLA Ops:
  0.6 1.0 %copy-start = (f32[2,16,4096]{2,1,0:T(8,128)S(1)}, f32[2,16,4096]{2,1,0:T(8,128)}, u32[]{:S(2)}) copy-start(f32[2,16,4096]{2,1,0:T(8,128)} %p_ref.1) | copy-start | bytes 1572868
  1.7 1.0 %copy-start.1 = (f32[2,16,4096]{2,1,0:T(8,128)S(1)}, f32[2,16,4096]{2,1,0:T(8,128)}, u32[]{:S(2)}) copy-start(f32[2,16,4096]{2,1,0:T(8,128)} %q_ref.1) | copy-start | bytes 1572868
  3.5 9.0 %collective-permute-start = (f32[4,96,128]{2,1,0:T(8,128)S(1)}, f32[4,96,128]{2,1,0:T(8,128)S(1)}, u32[]{:S(2)}, u32[]{:S(2)}) collective-permute-start(f32[4,96,128]{2,1,0:T(8,128)S(1)} %get-tuple-element.27), channel_id=1, source_target_pairs={{0,1},{1,0},{2,3},{3,2},{4,5},{5,4},{6,7},{7,6},{8,9},{9,8},{10,11... | collective-permute-start | bytes 589832 | tf_op jit(solution)/shard_map/ppermute | solution.py:577
  4.1 9.0 %collective-permute-start.1 = (f32[4,96,128]{2,1,0:T(8,128)S(1)}, f32[4,96,128]{2,1,0:T(8,128)S(1)}, u32[]{:S(2)}, u32[]{:S(2)}) collective-permute-start(f32[4,96,128]{2,1,0:T(8,128)S(1)} %get-tuple-element.28), channel_id=1, source_target_pairs={{1,2},{2,1},{3,4},{4,3},{5,6},{6,5},{7,8},{8,7},{9,10},{10,9},{11,... | collective-permute-start | bytes 589832 | tf_op jit(solution)/shard_map/ppermute | solution.py:577
  14.4 4.6 %collective-permute-start.2 = (f32[2,96,128]{2,1,0:T(8,128)S(1)}, f32[2,96,128]{2,1,0:T(8,128)S(1)}, u32[]{:S(2)}, u32[]{:S(2)}) collective-permute-start(f32[2,96,128]{2,1,0:T(8,128)S(1)} %get-tuple-element.31), channel_id=1, source_target_pairs={{0,1},{1,0},{2,3},{3,2},{4,5},{5,4},{6,7},{7,6},{8,9},{9,8},{10,11... | collective-permute-start | bytes 294920 | tf_op jit(solution)/shard_map/ppermute | solution.py:577
  14.4 6.8 %collective-permute-start.3 = (f32[2,96,128]{2,1,0:T(8,128)S(1)}, f32[2,96,128]{2,1,0:T(8,128)S(1)}, u32[]{:S(2)}, u32[]{:S(2)}) collective-permute-start(f32[2,96,128]{2,1,0:T(8,128)S(1)} %get-tuple-element.32), channel_id=1, source_target_pairs={{1,2},{2,1},{3,4},{4,3},{5,6},{6,5},{7,8},{8,7},{9,10},{10,9},{11,... | collective-permute-start | bytes 294920 | tf_op jit(solution)/shard_map/ppermute | solution.py:577
  33.5 2.9 %collective-permute-start.4 = (f32[8,2,32,128]{3,2,1,0:T(8,128)S(1)}, f32[8,2,32,128]{3,2,1,0:T(8,128)S(1)}, u32[]{:S(2)}, u32[]{:S(2)}) collective-permute-start(f32[8,2,32,128]{3,2,1,0:T(8,128)S(1)} %all_to_all.5.same_ref), channel_id=1, source_target_pairs={{0,1},{1,0},{2,3},{3,2},{4,5},{5,4},{6,7},{7,6},{8,9},{9,8},{10,11... | collective-permute-start | bytes 786440 | tf_op jit(solution)/shard_map/ppermute | solution.py:630

commit v3 on v2

--- a/solution.py
+++ b/solution.py
@@ -11,7 +11,8 @@
 LANES = 128
 SUBS = 8
 HALO = 3
-MID_HALO = 4
+MID_HALO = 6
+TWO_HALO = 4
 RELAX = 0.8
 COUPLING = (0.02, 0.04)
 TIME_STEP = 0.5
@@ -394,31 +395,70 @@
 
 
 def middle_kernel(
-    fine, level, coarse, rows, b_own, near_ref, far_ref, v0_in,
-    b_ref, v_ref, out_ref, v0_ref, v_one, bc,
+    fine, level, two, three, rows, b_own, near_ref, far_ref, v0_in,
+    b_ref, v_ref, b2_ref, v2_ref, out_ref, two_near_ref, two_far_ref, v0_ref,
+    v_one, w_two, b3,
 ):
     _, odd, is_first, is_last = place()
     total = rows + 2 * MID_HALO
+    own = rows // 2
     edge = MID_HALO * level.size
     b_ref[:, edge : edge + rows * level.size, :] = b_own[...]
     receive_edges(level, MID_HALO, MID_HALO, rows, b_ref, near_ref, far_ref)
     start(level, v_one, 0, b_ref, 0, 0, total, 4)
 
-    def trim(ref):
+    def trim(ref, of, halo, n):
         @pl.when(is_first)
         def _():
-            clear(ref, level, 0, MID_HALO)
+            clear(ref, of, 0, halo)
 
         @pl.when(is_last)
         def _():
-            clear(ref, level, MID_HALO + rows, total)
-
-    trim(v_one)
-    sweep(level, v_ref, 0, v_one, 0, b_ref, 0, 1, total - 1, 7)
-    trim(v_ref)
-    restrict(level, bc, 0, coarse, v_ref, MID_HALO, b_ref, MID_HALO, 0, rows // 2, 4)
-    for copy in range(out_ref.shape[0]):
-        out_ref[copy] = bc[...]
+            clear(ref, of, halo + n, 2 * halo + n)
+
+    trim(v_one, level, MID_HALO, rows)
+    sweep(level, v_ref, 0, v_one, 0, b_ref, 0, 1, total - 1, 6)
+    trim(v_ref, level, MID_HALO, rows)
+    restrict(
+        level, b2_ref, TWO_HALO, two, v_ref, MID_HALO, b_ref, MID_HALO, -2, own + 2, 4
+    )
+    start(two, w_two, TWO_HALO, b2_ref, TWO_HALO, -2, own + 2, 8)
+    trim(w_two, two, TWO_HALO, own)
+    sweep(two, v2_ref, TWO_HALO, w_two, TWO_HALO, b2_ref, TWO_HALO, -1, own + 1, 6)
+    trim(v2_ref, two, TWO_HALO, own)
+    restrict(
+        two, b3, 0, three, v2_ref, TWO_HALO, b2_ref, TWO_HALO, 0, own // 2, 2
+    )
+    even = lane_index() % 2 == 0
+    for layer in range(2):
+        for pair in range(own // 4):
+            row = jnp.where(
+                even,
+                b3[layer, at(three, 2 * pair), :],
+                b3[layer, at(three, 2 * pair + 1), :],
+            )
+            for copy in range(out_ref.shape[0]):
+                out_ref[copy, layer, at(three, pair), :] = row
+    up, down = pl.ds((TWO_HALO + 1) * two.size, 3 * two.size), pl.ds(
+        own * two.size, 3 * two.size
+    )
+    up_b, down_b = at(two, TWO_HALO + 2), at(two, TWO_HALO + own - 3)
+    last = pl.ds(3 * two.size, two.size)
+
+    def send(ref, rows_v, row_b):
+        ref[:, 0 : 3 * two.size, :] = v2_ref[:, rows_v, :]
+        ref[:, last, :] = b2_ref[:, row_b, :]
+
+    @pl.when(odd == 1)
+    def _():
+        send(two_near_ref, up, up_b)
+        send(two_far_ref, down, down_b)
+
+    @pl.when(odd == 0)
+    def _():
+        send(two_near_ref, down, down_b)
+        send(two_far_ref, up, up_b)
+
     top, low = (HALO - 2) * fine.size, (HALO + 2 * rows + 1) * fine.size
     near = pl.multiple_of(jnp.where(odd == 1, top, low), SUBS)
     far = pl.multiple_of(jnp.where(odd == 1, low, top), SUBS)
@@ -433,36 +473,66 @@
 
 
 def coarse_kernel(
-    levels, rows, same_ref, other_ref, b1_ref, v1_ref, b0_ref, v0_ref, out_ref,
-    b2, v2, w2, b3, v3, w3, b4, v4, w4, x1, y1, x0, y0, native, sems,
+    levels, rows, same_ref, other_ref, near_ref, far_ref,
+    b2_ref, v2_ref, b1_ref, v1_ref, b0_ref, v0_ref, out_ref,
+    b2, v2, x2, y2, b3, v3, w3, b4, v4, w4, x1, y1, x0, y0, native, sems,
 ):
     me, odd, is_first, is_last = place()
     fine, mid, two, three, four = levels
     own = rows // 4
     chips = same_ref.shape[0]
-    n2, n3, n4 = 2 * chips * own, chips * own, chips * own // 2
-    for ref, level, n in (
-        (b2, two, n2), (v2, two, n2), (w2, two, n2), (b3, three, n3), (v3, three, n3),
-        (w3, three, n3), (v4, four, n4), (w4, four, n4),
-    ):
+    n3, n4 = chips * own, chips * own // 2
+    for ref, level, n in ((b3, three, n3), (v3, three, n3), (w3, three, n3), (v4, four, n4), (w4, four, n4)):
         clear(ref, level, 0, PAD)
         clear(ref, level, PAD + n, 2 * PAD + n)
+    even = lane_index() % 2 == 0
 
     def gather_body(chip, carry):
         for ref, core in ((same_ref, odd), (other_ref, 1 - odd)):
-            row = pl.multiple_of(((2 * chip + core) * own + PAD) * two.size, SUBS)
-            b2[:, pl.ds(row, own * two.size), :] = ref[chip]
+            row = (2 * chip + core) * (own // 2) + PAD
+            for layer in range(2):
+                for pair in range(own // 4):
+                    both = ref[chip, layer, at(three, pair), :]
+                    first = jnp.where(even, both, pltpu.roll(both, 1, 1))
+                    second = jnp.where(even, pltpu.roll(both, LANES - 1, 1), both)
+                    b3[layer, at(three, row + 2 * pair), :] = first
+                    b3[layer, at(three, row + 2 * pair + 1), :] = second
         return carry
 
-    lax.fori_loop(0, chips, gather_body, 0, unroll=min(chips, 4))
-
-    start(two, v2, PAD, b2, PAD, 0, n2, 8)
-    sweep(two, w2, PAD, v2, PAD, b2, PAD, 0, n2, 8)
-    restrict(two, b3, PAD, three, w2, PAD, b2, PAD, 0, n3, 4)
+    lax.fori_loop(0, chips, gather_body, 0, unroll=min(chips, 8))
+
+    b2[...] = b2_ref[...]
+    v2[...] = v2_ref[...]
+
+    def take(ref, zero):
+        top_v, low_v = pl.ds(0, 3 * two.size), pl.ds((TWO_HALO + own + 1) * two.size, 3 * two.size)
+        top_b, low_b = at(two, TWO_HALO - 3), at(two, TWO_HALO + own + 2)
+        last = pl.ds(3 * two.size, two.size)
+
+        def put(rows_v, row_b):
+            values = ref[:, 0 : 3 * two.size, :]
+            v2[:, rows_v, :] = jnp.where(zero, 0.0, values) if zero is not None else values
+            b2[:, row_b, :] = ref[:, last, :]
+
+        return lambda: put(top_v, top_b), lambda: put(low_v, low_b)
+
+    near_top, near_low = take(near_ref, None)
+    far_top, far_low = take(far_ref, jnp.logical_or(is_first, is_last))
+
+    @pl.when(odd == 1)
+    def _():
+        near_top()
+        far_low()
+
+    @pl.when(odd == 0)
+    def _():
+        near_low()
+        far_top()
+
     start(three, v3, PAD, b3, PAD, 0, n3, 8)
-    sweep(three, w3, PAD, v3, PAD, b3, PAD, 0, n3, 8)
-    restrict(three, b4, 0, four, w3, PAD, b3, PAD, 0, n4, 4)
-    start(four, v4, PAD, b4, 0, 0, n4, 8)
+    sweep(three, w3, PAD, v3, PAD, b3, PAD, 0, n3, 16)
+    restrict(three, b4, 0, four, w3, PAD, b3, PAD, 0, n4, 8)
+    start(four, v4, PAD, b4, 0, 0, n4, 16)
     src, dst = v4, w4
     for _ in range(COARSE_SWEEPS - 1):
         sweep(four, dst, PAD, src, PAD, b4, 0, 0, n4, 16)
@@ -483,14 +553,6 @@
     trim(w3, three, n3)
     sweep(three, v3, PAD, w3, PAD, b3, PAD, me * half - 2, half + 4, 8)
     trim(v3, three, n3)
-    correct(two, three, v2, PAD, w2, PAD, v3, PAD, me * half - 2, half + 4, 8)
-    sweep(two, w2, PAD, v2, PAD, b2, PAD, me * own - 3, own + 6, 8)
-    trim(w2, two, n2)
-    sweep(two, v2, PAD, w2, PAD, b2, PAD, me * own - 2, own + 4, 8)
-    trim(v2, two, n2)
-
-    n1 = rows // 2
-    total = n1 + 2 * MID_HALO
 
     def trim_own(ref, level, halo, n):
         @pl.when(is_first)
@@ -501,12 +563,22 @@
         def _():
             clear(ref, level, halo + n, 2 * halo + n)
 
+    total = own + 2 * TWO_HALO
+    correct(two, three, x2, 0, v2, 0, v3, PAD + me * half - TWO_HALO // 2, 0, total // 2, 8)
+    sweep(two, y2, 0, x2, 0, b2, 0, 1, total - 1, 10)
+    trim_own(y2, two, TWO_HALO, own)
+    sweep(two, x2, 0, y2, 0, b2, 0, 2, total - 2, 8)
+    trim_own(x2, two, TWO_HALO, own)
+
+    n1 = rows // 2
+    total = n1 + 2 * MID_HALO
+
     correct(
-        mid, two, x1, 0, v1_ref, 0, v2, PAD + me * own - MID_HALO // 2, 0, total // 2, 4
+        mid, two, x1, MID_HALO - 4, v1_ref, MID_HALO - 4, x2, TWO_HALO - 2, 0, n1 // 2 + 4, 4
     )
-    sweep(mid, y1, 0, x1, 0, b1_ref, 0, 2, total - 2, 6)
+    sweep(mid, y1, 0, x1, 0, b1_ref, 0, MID_HALO - 2, MID_HALO + n1 + 2, 6)
     trim_own(y1, mid, MID_HALO, n1)
-    sweep(mid, x1, 0, y1, 0, b1_ref, 0, 3, total - 3, 5)
+    sweep(mid, x1, 0, y1, 0, b1_ref, 0, MID_HALO - 1, MID_HALO + n1 + 1, 5)
     trim_own(x1, mid, MID_HALO, n1)
 
     low, high = HALO, HALO + rows
@@ -614,34 +686,46 @@
         out_specs=HBM,
     )(b0)
     chips = count // 2
-    b1, v1, b2, v0 = call(
-        functools.partial(middle_kernel, fine, mid, two, half),
+    eighth = rows // 8
+    two_edge = shape(2, 4 * two.size, LANES)
+    two_all = shape(2, (quarter + 2 * TWO_HALO) * two.size, LANES)
+    b1, v1, b2, v2, b3, near, far, v0 = call(
+        functools.partial(middle_kernel, fine, mid, two, three, half),
         [
             shape(2, (half + 2 * MID_HALO) * mid.size, LANES),
             shape(2, (half + 2 * MID_HALO) * mid.size, LANES),
-            shape(chips, 2, quarter * two.size, LANES),
+            two_all,
+            two_all,
+            shape(chips, 2, eighth // 2 * three.size, LANES),
+            two_edge,
+            two_edge,
             shape(2, total * fine.size, LANES),
         ],
-        [scratch(2, half + 2 * MID_HALO, mid), scratch(2, quarter, two)],
-        input_output_aliases={3: 3},
+        [
+            scratch(2, half + 2 * MID_HALO, mid),
+            scratch(2, quarter + 2 * TWO_HALO, two),
+            scratch(2, eighth, three),
+        ],
+        input_output_aliases={3: 7},
     )(b1, near, far, v0)
+    near = lax.ppermute(near, "wide", core_swap)
+    far = lax.ppermute(far, "wide", chip_swap)
     cores = [[i for i in range(count) if i % 2 == c] for c in range(2)]
-    same = lax.all_to_all(b2, "wide", 0, 0, axis_index_groups=cores)
+    same = lax.all_to_all(b3, "wide", 0, 0, axis_index_groups=cores)
     other = lax.ppermute(same, "wide", core_swap)
-    n2, n3, n4 = count * quarter, count * quarter // 2, count * quarter // 4
+    n3, n4 = count * eighth, count * eighth // 2
     stream_next = call(
         functools.partial(coarse_kernel, (fine, mid, two, three, four), rows),
         shape(2, rows, columns),
-        [scratch(2, n2 + 2 * PAD, two)] * 3
+        [scratch(2, quarter + 2 * TWO_HALO, two)] * 4
         + [scratch(2, n3 + 2 * PAD, three)] * 3
         + [scratch(2, n4, four)]
         + [scratch(2, n4 + 2 * PAD, four)] * 2
         + [scratch(2, half + 2 * MID_HALO, mid)] * 2
         + [scratch(2, total, fine)] * 2
         + [pltpu.VMEM((2, rows, columns), jnp.float32), pltpu.SemaphoreType.DMA((2, groups))],
-        limit=40,
         out_specs=HBM,
-    )(same, other, b1, v1, b0, v0)
+    )(same, other, near, far, b2, v2, b1, v1, b0, v0)
     return (vorticity_next, stream_next)
 
 

time: 44.7 us -> 45.9 us (1.027)
  waiting for transfers between devices: 2.96 us -> 7.25 us
  Pallas kernels: 14.6 us -> 12.5 us
  blocking collectives: 11.6 us -> 10 us
  starting transfers between devices: 12.5 us -> 13.1 us
    ppermute x0 -> x2, waiting for transfers between devices: none -> 4.05 us  [the longest x1 4.05 us: shards(): far = lax.ppermute(far, 'wide', chip_swap)]
    pallas_call x1, Pallas kernels: 8.11 us -> 5.31 us  [shards(): call(functools.partial(coarse_kernel, (fine, mid, two, three, four), rows...]
    all_to_all x1, blocking collectives: 11.6 us -> 10 us  [shards(): same = lax.all_to_all(b3, 'wide', 0, 0, axis_index_groups=cores)]
    ppermute x0 -> x2, starting transfers between devices: none -> 0.94 us  [the longest x1 0.94 us: shards(): far = lax.ppermute(far, 'wide', chip_swap)]
    pallas_call x1, Pallas kernels: 0.62 us -> 1.33 us  [shards(): call(functools.partial(middle_kernel, fine, mid, two, three, half), [shap...]
  transfers between devices with their start and end apart: 5 -> 7, of which waited for: 3 -> 3; matrix products, arithmetic and copies ran while one was open for 0% -> 0% of each run, Pallas kernels for 9% -> 8%
where the time goes in v3:
time: 45.9 us; the launch traced here: 45.7 us
  starting transfers between devices  13.1 us (29%)
  Pallas kernels  12.5 us (27%)
  blocking collectives  10 us (22%)
  waiting for transfers between devices  7.25 us (16%)
  local copies, waits for them, and re-layouts  2.08 us (5%)
  between operations  0.7 us (2%)
    ppermute x2, starting transfers between devices, exchange(): lax.ppermute(far, 'wide', chip_swap)  10.2 us
    all_to_all x1, blocking collectives, shards(): same = lax.all_to_all(b3, 'wide', 0, 0, axis_index_groups=cores)  10 us
    pallas_call x1, Pallas kernels, shards(): call(functools.partial(coarse_kernel, (fine, mid, two, three, four), rows...  5.31 us
    ppermute x1, waiting for transfers between devices, shards(): far = lax.ppermute(far, 'wide', chip_swap)  4.05 us
    ppermute x2, waiting for transfers between devices, exchange(): lax.ppermute(far, 'wide', chip_swap)  3.18 us
    pallas_call x1, Pallas kernels, shards(): call(functools.partial(inner_kernel, fine, mid, rows), state, cost=8000000)  2.8 us
    unnamed x4, local copies, waits for them, and re-layouts  2.08 us
    ppermute x1, starting transfers between devices, shards(): other = lax.ppermute(same, 'wide', core_swap)  1.35 us
  transfers between devices with their start and end apart: 7, of which 3 were waited for; matrix products, arithmetic and copies ran while one was open for 0% of the time, Pallas kernels for 8%

profile of v3, /device:TPU:0, one launch (start us, length us, event | category | flops | bytes accessed | tf_op | source)
XLA Modules:
  0.0 45.7 jit_solution(5907553810965532961)
XLA Ops:
  0.6 0.0 copy-start
  0.6 1.0 %copy-done = f32[2,16,4096]{2,1,0:T(8,128)S(1)} copy-done((f32[2,16,4096]{2,1,0:T(8,128)S(1)}, f32[2,16,4096]{2,1,0:T(8,128)}, u32[]{:S(2)}) %copy-start) | copy-done | bytes 524312
  1.7 1.0 %copy-done.1 = f32[2,16,4096]{2,1,0:T(8,128)S(1)} copy-done((f32[2,16,4096]{2,1,0:T(8,128)S(1)}, f32[2,16,4096]{2,1,0:T(8,128)}, u32[]{:S(2)}) %copy-start.1) | copy-done | bytes 524312
  2.7 0.8 %shard_map.41 = (f32[4,704,128]{2,1,0:T(8,128)S(1)}, f32[4,96,128]{2,1,0:T(8,128)S(1)}, f32[4,96,128]{2,1,0:T(8,128)S(1)}) custom-call(f32[2,16,4096]{2,1,0:T(8,128)S(1)} %copy-done, f32[2,16,4096]{2,1,0:T(8,128)S(1)} %copy-done.1), custom_call_target="tpu_custom_call" | custom-call | tf_op jit(solution)/shard_map/pallas_call | solution.py:653
  3.5 0.6 %collective-permute-start = (f32[4,96,128]{2,1,0:T(8,128)S(1)}, f32[4,96,128]{2,1,0:T(8,128)S(1)}, u32[]{:S(2)}, u32[]{:S(2)}) collective-permute-start(f32[4,96,128]{2,1,0:T(8,128)S(1)} %get-tuple-element.31), channel_id=1, source_target_pairs={{0,1},{1,0},{2,3},{3,2},{4,5},{5,4},{6,7},{7,6},{8,9},{9,8},{10,11... | collective-permute-start | bytes 589832 | tf_op jit(solution)/shard_map/ppermute | solution.py:649
  4.1 5.7 %collective-permute-start.1 = (f32[4,96,128]{2,1,0:T(8,128)S(1)}, f32[4,96,128]{2,1,0:T(8,128)S(1)}, u32[]{:S(2)}, u32[]{:S(2)}) collective-permute-start(f32[4,96,128]{2,1,0:T(8,128)S(1)} %get-tuple-element.32), channel_id=1, source_target_pairs={{1,2},{2,1},{3,4},{4,3},{5,6},{6,5},{7,8},{8,7},{9,10},{10,9},{11,... | collective-permute-start | bytes 589832 | tf_op jit(solution)/shard_map/ppermute | solution.py:649
  9.7 2.8 %shard_map.42 = (f32[4,704,128]{2,1,0:T(8,128)S(1)}, f32[4,704,128]{2,1,0:T(8,128)S(1)}, f32[2,704,128]{2,1,0:T(8,128)S(1)}, f32[2,704,128]{2,1,0:T(8,128)S(1)},...) custom-call(f32[4,704,128]{2,1,0:T(8,128)S(1)} %get-tuple-element.24.ext.refs_0_), custom_call_target="tpu_custom_call" | custom-call | flops 8000000 | bytes 1000000 | tf_op jit(solution)/shard_map/pallas_call | solution.py:668
  12.5 0.0 collective-permute-done.refs_7_
  12.5 0.5 %collective-permute-done.1.refs_8_ = f32[4,96,128]{2,1,0:T(8,128)S(1)} collective-permute-done((f32[4,96,128]{2,1,0:T(8,128)S(1)}, f32[4,96,128]{2,1,0:T(8,128)S(1)}, u32[]{:S(2)}, u32[]{:S(2)}) %collective-permute-start.1) | collective-permute-done | bytes 196640 | tf_op jit(solution)/shard_map/ppermute | solution.py:649
  13.1 1.3 %shard_map.43 = (f32[4,704,128]{2,1,0:T(8,128)S(1)}, f32[4,704,128]{2,1,0:T(8,128)S(1)}, f32[4,704,128]{2,1,0:T(8,128)S(1)}, f32[2,704,128]{2,1,0:T(8,128)S(1)},...) custom-call(f32[4,704,128]{2,1,0:T(8,128)S(1)} %get-tuple-element.24, ...), custom_call_target="tpu_custom_call", output_to_operand_aliasing={{0}: (0, {}), {1}: (1, {}), {2}: (2, {}), {3}: (3, {}), {4}... | custom-call | tf_op jit(solution)/shard_map/pallas_call | solution.py:674
  14.4 0.1 collective-permute-start.2
  14.4 4.5 %collective-permute-start.3 = (f32[2,128,128]{2,1,0:T(8,128)S(1)}, f32[2,128,128]{2,1,0:T(8,128)S(1)}, u32[]{:S(2)}, u32[]{:S(2)}) collective-permute-start(f32[2,128,128]{2,1,0:T(8,128)S(1)} %get-tuple-element.36), channel_id=1, source_target_pairs={{1,2},{2,1},{3,4},{4,3},{5,6},{6,5},{7,8},{8,7},{9,10},{10,9},{11,... | collective-permute-start | bytes 393224 | tf_op jit(solution)/shard_map/ppermute | solution.py:649
  18.9 0.0 collective-permute-done.2.near_ref
  18.9 2.6 %collective-permute-done.3.far_ref = f32[2,128,128]{2,1,0:T(8,128)S(1)} collective-permute-done((f32[2,128,128]{2,1,0:T(8,128)S(1)}, f32[2,128,128]{2,1,0:T(8,128)S(1)}, u32[]{:S(2)}, u32[]{:S(2)}) %collective-permute-start.3) | collective-permute-done | bytes 131104 | tf_op jit(solution)/shard_map/ppermute | solution.py:649
  21.6 1.3 %shard_map.45 = (f32[2,320,128]{2,1,0:T(8,128)S(1)}, f32[2,320,128]{2,1,0:T(8,128)S(1)}, f32[2,96,128]{2,1,0:T(8,128)S(1)}, f32[2,96,128]{2,1,0:T(8,128)S(1)}, f...) custom-call(f32[2,128,128]{2,1,0:T(8,128)S(1)} %get-tuple-element.34, ...), custom_call_target="tpu_custom_call", output_to_operand_aliasing={{7}: (3, {})} | custom-call | tf_op jit(solution)/shard_map/pallas_call | solution.py:692
  22.9 10.0 %all_to_all.5.same_ref = f32[8,2,8,128]{3,2,1,0:T(8,128)S(1)} all-to-all(f32[8,2,8,128]{3,2,1,0:T(8,128)S(1)} %get-tuple-element.38), channel_id=1, replica_groups={{0,2,4,6,8,10,12,14},{1,3,5,7,9,11,13,15},{16,18,20,22,24,26,28,30},{17..., dimensions={0} | all-to-all | bytes 131072 | tf_op jit(solution)/shard_map/all_to_all | solution.py:714
  33.0 1.4 %collective-permute-start.4 = (f32[8,2,8,128]{3,2,1,0:T(8,128)S(1)}, f32[8,2,8,128]{3,2,1,0:T(8,128)S(1)}, u32[]{:S(2)}, u32[]{:S(2)}) collective-permute-start(f32[8,2,8,128]{3,2,1,0:T(8,128)S(1)} %all_to_all.5.same_ref), channel_id=1, source_target_pairs={{0,1},{1,0},{2,3},{3,2},{4,5},{5,4},{6,7},{7,6},{8,9},{9,8},{10,11... | collective-permute-start | bytes 196616 | tf_op jit(solution)/shard_map/ppermute | solution.py:715
  34.3 0.0 collective-permute-start.5
  34.3 0.9 %collective-permute-start.6 = (f32[2,32,128]{2,1,0:T(8,128)S(1)}, f32[2,32,128]{2,1,0:T(8,128)S(1)}, u32[]{:S(2)}, u32[]{:S(2)}) collective-permute-start(f32[2,32,128]{2,1,0:T(8,128)S(1)} %get-tuple-element.40), channel_id=1, source_target_pairs={{1,2},{2,1},{3,4},{4,3},{5,6},{6,5},{7,8},{8,7},{9,10},{10,9},{11,... | collective-permute-start | bytes 98312 | tf_op jit(solution)/shard_map/ppermute | solution.py:712
  35.3 1.0 %shard_map.44 = f32[2,16,4096]{2,1,0:T(8,128)} custom-call(f32[2,704,128]{2,1,0:T(8,128)S(1)} %get-tuple-element.33.b_ref.b0_ref), custom_call_target="tpu_custom_call" | custom-call | flops 4000000 | bytes 500000 | tf_op jit(solution)/shard_map/pallas_call | solution.py:681
  36.3 0.0 collective-permute-done.5.near_ref
  36.3 4.1 %collective-permute-done.6.far_ref = f32[2,32,128]{2,1,0:T(8,128)S(1)} collective-permute-done((f32[2,32,128]{2,1,0:T(8,128)S(1)}, f32[2,32,128]{2,1,0:T(8,128)S(1)}, u32[]{:S(2)}, u32[]{:S(2)}) %collective-permute-start.6) | collective-permute-done | bytes 32800 | tf_op jit(solution)/shard_map/ppermute | solution.py:712
  40.4 0.0 collective-permute-done.4.other_ref
  40.4 5.3 %shard_map.46 = f32[2,16,4096]{2,1,0:T(8,128)} custom-call(f32[8,2,8,128]{3,2,1,0:T(8,128)S(1)} %all_to_all.5.same_ref, f32[8,2,8,128]{3,2,1,0:T(8,128)S(1)} %collective-permute-done.4.other_ref, f32[2,32,128]{2,1,0:T(8,128)S(1)} %collective-permute-done.5.near_ref, f32[2,32,128]{2,1,0:T(8,128)S(1)} %collective-permute-done.6.far_ref, ...), custom_call_target="tpu_custom_call" | custom-call | tf_op jit(solution)/shard_map/pallas_call | solution.py:717
  (1 shorter events, 0.0 us)
Async XLA Ops:
  0.6 1.0 %copy-start = (f32[2,16,4096]{2,1,0:T(8,128)S(1)}, f32[2,16,4096]{2,1,0:T(8,128)}, u32[]{:S(2)}) copy-start(f32[2,16,4096]{2,1,0:T(8,128)} %p_ref.1) | copy-start | bytes 1572868
  1.7 1.0 %copy-start.1 = (f32[2,16,4096]{2,1,0:T(8,128)S(1)}, f32[2,16,4096]{2,1,0:T(8,128)}, u32[]{:S(2)}) copy-start(f32[2,16,4096]{2,1,0:T(8,128)} %q_ref.1) | copy-start | bytes 1572868
  3.5 9.0 %collective-permute-start = (f32[4,96,128]{2,1,0:T(8,128)S(1)}, f32[4,96,128]{2,1,0:T(8,128)S(1)}, u32[]{:S(2)}, u32[]{:S(2)}) collective-permute-start(f32[4,96,128]{2,1,0:T(8,128)S(1)} %get-tuple-element.31), channel_id=1, source_target_pairs={{0,1},{1,0},{2,3},{3,2},{4,5},{5,4},{6,7},{7,6},{8,9},{9,8},{10,11... | collective-permute-start | bytes 589832 | tf_op jit(solution)/shard_map/ppermute | solution.py:649
  4.1 9.0 %collective-permute-start.1 = (f32[4,96,128]{2,1,0:T(8,128)S(1)}, f32[4,96,128]{2,1,0:T(8,128)S(1)}, u32[]{:S(2)}, u32[]{:S(2)}) collective-permute-start(f32[4,96,128]{2,1,0:T(8,128)S(1)} %get-tuple-element.32), channel_id=1, source_target_pairs={{1,2},{2,1},{3,4},{4,3},{5,6},{6,5},{7,8},{8,7},{9,10},{10,9},{11,... | collective-permute-start | bytes 589832 | tf_op jit(solution)/shard_map/ppermute | solution.py:649
  14.4 4.6 %collective-permute-start.2 = (f32[2,128,128]{2,1,0:T(8,128)S(1)}, f32[2,128,128]{2,1,0:T(8,128)S(1)}, u32[]{:S(2)}, u32[]{:S(2)}) collective-permute-start(f32[2,128,128]{2,1,0:T(8,128)S(1)} %get-tuple-element.35), channel_id=1, source_target_pairs={{0,1},{1,0},{2,3},{3,2},{4,5},{5,4},{6,7},{7,6},{8,9},{9,8},{10,11... | collective-permute-start | bytes 393224 | tf_op jit(solution)/shard_map/ppermute | solution.py:649
  14.4 7.2 %collective-permute-start.3 = (f32[2,128,128]{2,1,0:T(8,128)S(1)}, f32[2,128,128]{2,1,0:T(8,128)S(1)}, u32[]{:S(2)}, u32[]{:S(2)}) collective-permute-start(f32[2,128,128]{2,1,0:T(8,128)S(1)} %get-tuple-element.36), channel_id=1, source_target_pairs={{1,2},{2,1},{3,4},{4,3},{5,6},{6,5},{7,8},{8,7},{9,10},{10,9},{11,... | collective-permute-start | bytes 393224 | tf_op jit(solution)/shard_map/ppermute | solution.py:649
  33.0 7.4 %collective-permute-start.4 = (f32[8,2,8,128]{3,2,1,0:T(8,128)S(1)}, f32[8,2,8,128]{3,2,1,0:T(8,128)S(1)}, u32[]{:S(2)}, u32[]{:S(2)}) collective-permute-start(f32[8,2,8,128]{3,2,1,0:T(8,128)S(1)} %all_to_all.5.same_ref), channel_id=1, source_target_pairs={{0,1},{1,0},{2,3},{3,2},{4,5},{5,4},{6,7},{7,6},{8,9},{9,8},{10,11... | collective-permute-start | bytes 196616 | tf_op jit(solution)/shard_map/ppermute | solution.py:715
  34.3 2.0 %collective-permute-start.5 = (f32[2,32,128]{2,1,0:T(8,128)S(1)}, f32[2,32,128]{2,1,0:T(8,128)S(1)}, u32[]{:S(2)}, u32[]{:S(2)}) collective-permute-start(f32[2,32,128]{2,1,0:T(8,128)S(1)} %get-tuple-element.39), channel_id=1, source_target_pairs={{0,1},{1,0},{2,3},{3,2},{4,5},{5,4},{6,7},{7,6},{8,9},{9,8},{10,11... | collective-permute-start | bytes 98312 | tf_op jit(solution)/shard_map/ppermute | solution.py:711
  34.3 6.0 %collective-permute-start.6 = (f32[2,32,128]{2,1,0:T(8,128)S(1)}, f32[2,32,128]{2,1,0:T(8,128)S(1)}, u32[]{:S(2)}, u32[]{:S(2)}) collective-permute-start(f32[2,32,128]{2,1,0:T(8,128)S(1)} %get-tuple-element.40), channel_id=1, source_target_pairs={{1,2},{2,1},{3,4},{4,3},{5,6},{6,5},{7,8},{8,7},{9,10},{10,9},{11,... | collective-permute-start | bytes 98312 | tf_op jit(solution)/shard_map/ppermute | solution.py:712

commit v4 on v3

--- a/solution.py
+++ b/solution.py
@@ -641,12 +641,20 @@
     fine, mid = Level(0, tiles, 1), Level(1, tiles // 2, 1)
     two, three, four = Level(2, tiles // 4, 1), Level(3, tiles // 4, 2), Level(4, tiles // 4, 4)
     core_swap = [(i, i ^ 1) for i in range(count)]
-    chip_swap = [(i, ((i + 1) ^ 1) - 1) for i in range(1, count - 1)]
-    chip_swap += [(0, count - 1), (count - 1, 0)]
+    members = lax.axis_size("member")
+    inside = [(i, ((i + 1) ^ 1) - 1) for i in range(1, count - 1)]
+    if members % 2:
+        ends = [(0, count - 1), (count - 1, 0)]
+        chip_swap = [(m * count + i, m * count + j) for m in range(members) for i, j in ends]
+    else:
+        chip_swap = [
+            (m * count + i, (m ^ 1) * count + i) for m in range(members) for i in (0, count - 1)
+        ]
+    chip_swap += [(m * count + i, m * count + j) for m in range(members) for i, j in inside]
     groups = rows // SUBS
 
     def exchange(near, far):
-        return lax.ppermute(near, "wide", core_swap), lax.ppermute(far, "wide", chip_swap)
+        return lax.ppermute(near, "wide", core_swap), lax.ppermute(far, ("member", "wide"), chip_swap)
 
     half, quarter = rows // 2, rows // 4
     total = rows + 2 * HALO
@@ -709,7 +717,7 @@
         input_output_aliases={3: 7},
     )(b1, near, far, v0)
     near = lax.ppermute(near, "wide", core_swap)
-    far = lax.ppermute(far, "wide", chip_swap)
+    far = lax.ppermute(far, ("member", "wide"), chip_swap)
     cores = [[i for i in range(count) if i % 2 == c] for c in range(2)]
     same = lax.all_to_all(b3, "wide", 0, 0, axis_index_groups=cores)
     other = lax.ppermute(same, "wide", core_swap)

time: 45.9 us -> 42.4 us (0.924)
  starting transfers between devices: 13.1 us -> 7.87 us
  blocking collectives: 10 us -> 13.3 us
  waiting for transfers between devices: 7.25 us -> 5.69 us
    ppermute x3, starting transfers between devices: 11.1 us -> 5.53 us  [the longest x2 4.04 us: exchange(): lax.ppermute(far, ('member', 'wide'), chip_swap)]
    all_to_all x1, blocking collectives: 10 us -> 13.3 us  [shards(): same = lax.all_to_all(b3, 'wide', 0, 0, axis_index_groups=cores)]
    ppermute x3, waiting for transfers between devices: 7.23 us -> 5.68 us  [the longest x2 4.3 us: exchange(): lax.ppermute(far, ('member', 'wide'), chip_swap)]
    ppermute x1, starting transfers between devices: 1.35 us -> 0.01 us  [shards(): other = lax.ppermute(same, 'wide', core_swap)]
    ppermute x2, starting transfers between devices: 0.63 us -> 1.83 us  [exchange(): lax.ppermute(near, 'wide', core_swap)]
    ppermute x1, starting transfers between devices: 0.01 us -> 0.51 us  [shards(): near = lax.ppermute(near, 'wide', core_swap)]
  transfers between devices with their start and end apart: 7 -> 7, of which waited for: 3 -> 3; matrix products, arithmetic and copies ran while one was open for 0% -> 0% of each run, Pallas kernels for 8% -> 9%
where the time goes in v4:
time: 42.4 us; the launch traced here: 42.1 us
  blocking collectives  13.3 us (31%)
  Pallas kernels  12.5 us (29%)
  starting transfers between devices  7.87 us (19%)
  waiting for transfers between devices  5.69 us (13%)
  local copies, waits for them, and re-layouts  2.08 us (5%)
  between operations  0.69 us (2%)
    all_to_all x1, blocking collectives, shards(): same = lax.all_to_all(b3, 'wide', 0, 0, axis_index_groups=cores)  13.3 us
    pallas_call x1, Pallas kernels, shards(): call(functools.partial(coarse_kernel, (fine, mid, two, three, four), rows...  5.31 us
    ppermute x2, waiting for transfers between devices, exchange(): lax.ppermute(far, ('member', 'wide'), chip_swap)  4.3 us
    ppermute x2, starting transfers between devices, exchange(): lax.ppermute(far, ('member', 'wide'), chip_swap)  4.04 us
    pallas_call x1, Pallas kernels, shards(): call(functools.partial(inner_kernel, fine, mid, rows), state, cost=8000000)  2.8 us
    unnamed x4, local copies, waits for them, and re-layouts  2.08 us
    ppermute x2, starting transfers between devices, exchange(): lax.ppermute(near, 'wide', core_swap)  1.83 us
    ppermute x1, starting transfers between devices, shards(): far = lax.ppermute(far, ('member', 'wide'), chip_swap)  1.49 us
  transfers between devices with their start and end apart: 7, of which 3 were waited for; matrix products, arithmetic and copies ran while one was open for 0% of the time, Pallas kernels for 9%

profile of v4, /device:TPU:0, one launch (start us, length us, event | category | flops | bytes accessed | tf_op | source)
XLA Modules:
  0.0 42.1 jit_solution(2222572757046661745)
XLA Ops:
  0.6 0.0 copy-start
  0.6 1.0 %copy-done = f32[2,16,4096]{2,1,0:T(8,128)S(1)} copy-done((f32[2,16,4096]{2,1,0:T(8,128)S(1)}, f32[2,16,4096]{2,1,0:T(8,128)}, u32[]{:S(2)}) %copy-start) | copy-done | bytes 524312
  1.7 1.0 %copy-done.1 = f32[2,16,4096]{2,1,0:T(8,128)S(1)} copy-done((f32[2,16,4096]{2,1,0:T(8,128)S(1)}, f32[2,16,4096]{2,1,0:T(8,128)}, u32[]{:S(2)}) %copy-start.1) | copy-done | bytes 524312
  2.7 0.8 %shard_map.41 = (f32[4,704,128]{2,1,0:T(8,128)S(1)}, f32[4,96,128]{2,1,0:T(8,128)S(1)}, f32[4,96,128]{2,1,0:T(8,128)S(1)}) custom-call(f32[2,16,4096]{2,1,0:T(8,128)S(1)} %copy-done, f32[2,16,4096]{2,1,0:T(8,128)S(1)} %copy-done.1), custom_call_target="tpu_custom_call" | custom-call | tf_op jit(solution)/shard_map/pallas_call | solution.py:661
  3.5 0.6 %collective-permute-start = (f32[4,96,128]{2,1,0:T(8,128)S(1)}, f32[4,96,128]{2,1,0:T(8,128)S(1)}, u32[]{:S(2)}, u32[]{:S(2)}) collective-permute-start(f32[4,96,128]{2,1,0:T(8,128)S(1)} %get-tuple-element.31), channel_id=1, source_target_pairs={{0,1},{1,0},{2,3},{3,2},{4,5},{5,4},{6,7},{7,6},{8,9},{9,8},{10,11... | collective-permute-start | bytes 589832 | tf_op jit(solution)/shard_map/ppermute | solution.py:657
  4.1 2.6 %collective-permute-start.1 = (f32[4,96,128]{2,1,0:T(8,128)S(1)}, f32[4,96,128]{2,1,0:T(8,128)S(1)}, u32[]{:S(2)}, u32[]{:S(2)}) collective-permute-start(f32[4,96,128]{2,1,0:T(8,128)S(1)} %get-tuple-element.32), channel_id=1, source_target_pairs={{0,16},{15,31},{16,0},{31,15},{1,2},{2,1},{3,4},{4,3},{5,6},{6,5},... | collective-permute-start | bytes 589832 | tf_op jit(solution)/shard_map/ppermute | solution.py:657
  6.6 2.8 %shard_map.42 = (f32[4,704,128]{2,1,0:T(8,128)S(1)}, f32[4,704,128]{2,1,0:T(8,128)S(1)}, f32[2,704,128]{2,1,0:T(8,128)S(1)}, f32[2,704,128]{2,1,0:T(8,128)S(1)},...) custom-call(f32[4,704,128]{2,1,0:T(8,128)S(1)} %get-tuple-element.24.ext.refs_0_), custom_call_target="tpu_custom_call" | custom-call | flops 8000000 | bytes 1000000 | tf_op jit(solution)/shard_map/pallas_call | solution.py:676
  9.4 0.0 collective-permute-done.refs_7_
  9.4 0.8 %collective-permute-done.1.refs_8_ = f32[4,96,128]{2,1,0:T(8,128)S(1)} collective-permute-done((f32[4,96,128]{2,1,0:T(8,128)S(1)}, f32[4,96,128]{2,1,0:T(8,128)S(1)}, u32[]{:S(2)}, u32[]{:S(2)}) %collective-permute-start.1) | collective-permute-done | bytes 196640 | tf_op jit(solution)/shard_map/ppermute | solution.py:657
  10.3 1.3 %shard_map.43 = (f32[4,704,128]{2,1,0:T(8,128)S(1)}, f32[4,704,128]{2,1,0:T(8,128)S(1)}, f32[4,704,128]{2,1,0:T(8,128)S(1)}, f32[2,704,128]{2,1,0:T(8,128)S(1)},...) custom-call(f32[4,704,128]{2,1,0:T(8,128)S(1)} %get-tuple-element.24, ...), custom_call_target="tpu_custom_call", output_to_operand_aliasing={{0}: (0, {}), {1}: (1, {}), {2}: (2, {}), {3}: (3, {}), {4}... | custom-call | tf_op jit(solution)/shard_map/pallas_call | solution.py:682
  11.5 1.3 %collective-permute-start.2 = (f32[2,128,128]{2,1,0:T(8,128)S(1)}, f32[2,128,128]{2,1,0:T(8,128)S(1)}, u32[]{:S(2)}, u32[]{:S(2)}) collective-permute-start(f32[2,128,128]{2,1,0:T(8,128)S(1)} %get-tuple-element.35), channel_id=1, source_target_pairs={{0,1},{1,0},{2,3},{3,2},{4,5},{5,4},{6,7},{7,6},{8,9},{9,8},{10,11... | collective-permute-start | bytes 393224 | tf_op jit(solution)/shard_map/ppermute | solution.py:657
  12.8 1.5 %collective-permute-start.3 = (f32[2,128,128]{2,1,0:T(8,128)S(1)}, f32[2,128,128]{2,1,0:T(8,128)S(1)}, u32[]{:S(2)}, u32[]{:S(2)}) collective-permute-start(f32[2,128,128]{2,1,0:T(8,128)S(1)} %get-tuple-element.36), channel_id=1, source_target_pairs={{0,16},{15,31},{16,0},{31,15},{1,2},{2,1},{3,4},{4,3},{5,6},{6,5},... | collective-permute-start | bytes 393224 | tf_op jit(solution)/shard_map/ppermute | solution.py:657
  14.3 0.0 collective-permute-done.2.near_ref
  14.3 3.5 %collective-permute-done.3.far_ref = f32[2,128,128]{2,1,0:T(8,128)S(1)} collective-permute-done((f32[2,128,128]{2,1,0:T(8,128)S(1)}, f32[2,128,128]{2,1,0:T(8,128)S(1)}, u32[]{:S(2)}, u32[]{:S(2)}) %collective-permute-start.3) | collective-permute-done | bytes 131104 | tf_op jit(solution)/shard_map/ppermute | solution.py:657
  17.8 1.3 %shard_map.45 = (f32[2,320,128]{2,1,0:T(8,128)S(1)}, f32[2,320,128]{2,1,0:T(8,128)S(1)}, f32[2,96,128]{2,1,0:T(8,128)S(1)}, f32[2,96,128]{2,1,0:T(8,128)S(1)}, f...) custom-call(f32[2,128,128]{2,1,0:T(8,128)S(1)} %get-tuple-element.34, ...), custom_call_target="tpu_custom_call", output_to_operand_aliasing={{7}: (3, {})} | custom-call | tf_op jit(solution)/shard_map/pallas_call | solution.py:700
  19.1 13.3 %all_to_all.5.same_ref = f32[8,2,8,128]{3,2,1,0:T(8,128)S(1)} all-to-all(f32[8,2,8,128]{3,2,1,0:T(8,128)S(1)} %get-tuple-element.38), channel_id=1, replica_groups={{0,2,4,6,8,10,12,14},{1,3,5,7,9,11,13,15},{16,18,20,22,24,26,28,30},{17..., dimensions={0} | all-to-all | bytes 131072 | tf_op jit(solution)/shard_map/all_to_all | solution.py:722
  32.4 0.0 collective-permute-start.4
  32.4 0.5 %collective-permute-start.5 = (f32[2,32,128]{2,1,0:T(8,128)S(1)}, f32[2,32,128]{2,1,0:T(8,128)S(1)}, u32[]{:S(2)}, u32[]{:S(2)}) collective-permute-start(f32[2,32,128]{2,1,0:T(8,128)S(1)} %get-tuple-element.39), channel_id=1, source_target_pairs={{0,1},{1,0},{2,3},{3,2},{4,5},{5,4},{6,7},{7,6},{8,9},{9,8},{10,11... | collective-permute-start | bytes 98312 | tf_op jit(solution)/shard_map/ppermute | solution.py:719
  32.9 1.5 %collective-permute-start.6 = (f32[2,32,128]{2,1,0:T(8,128)S(1)}, f32[2,32,128]{2,1,0:T(8,128)S(1)}, u32[]{:S(2)}, u32[]{:S(2)}) collective-permute-start(f32[2,32,128]{2,1,0:T(8,128)S(1)} %get-tuple-element.40), channel_id=1, source_target_pairs={{0,16},{15,31},{16,0},{31,15},{1,2},{2,1},{3,4},{4,3},{5,6},{6,5},... | collective-permute-start | bytes 98312 | tf_op jit(solution)/shard_map/ppermute | solution.py:720
  34.4 1.0 %shard_map.44 = f32[2,16,4096]{2,1,0:T(8,128)} custom-call(f32[2,704,128]{2,1,0:T(8,128)S(1)} %get-tuple-element.33.b_ref.b0_ref), custom_call_target="tpu_custom_call" | custom-call | flops 4000000 | bytes 500000 | tf_op jit(solution)/shard_map/pallas_call | solution.py:689
  35.4 0.0 collective-permute-done.5.near_ref
  35.5 1.4 %collective-permute-done.6.far_ref = f32[2,32,128]{2,1,0:T(8,128)S(1)} collective-permute-done((f32[2,32,128]{2,1,0:T(8,128)S(1)}, f32[2,32,128]{2,1,0:T(8,128)S(1)}, u32[]{:S(2)}, u32[]{:S(2)}) %collective-permute-start.6) | collective-permute-done | bytes 32800 | tf_op jit(solution)/shard_map/ppermute | solution.py:720
  36.8 0.0 collective-permute-done.4.other_ref
  36.8 5.3 %shard_map.46 = f32[2,16,4096]{2,1,0:T(8,128)} custom-call(f32[8,2,8,128]{3,2,1,0:T(8,128)S(1)} %all_to_all.5.same_ref, f32[8,2,8,128]{3,2,1,0:T(8,128)S(1)} %collective-permute-done.4.other_ref, f32[2,32,128]{2,1,0:T(8,128)S(1)} %collective-permute-done.5.near_ref, f32[2,32,128]{2,1,0:T(8,128)S(1)} %collective-permute-done.6.far_ref, ...), custom_call_target="tpu_custom_call" | custom-call | tf_op jit(solution)/shard_map/pallas_call | solution.py:725
  (1 shorter events, 0.0 us)
Async XLA Ops:
  0.6 1.0 %copy-start = (f32[2,16,4096]{2,1,0:T(8,128)S(1)}, f32[2,16,4096]{2,1,0:T(8,128)}, u32[]{:S(2)}) copy-start(f32[2,16,4096]{2,1,0:T(8,128)} %p_ref.1) | copy-start | bytes 1572868
  1.7 1.0 %copy-start.1 = (f32[2,16,4096]{2,1,0:T(8,128)S(1)}, f32[2,16,4096]{2,1,0:T(8,128)}, u32[]{:S(2)}) copy-start(f32[2,16,4096]{2,1,0:T(8,128)} %q_ref.1) | copy-start | bytes 1572868
  3.5 5.9 %collective-permute-start = (f32[4,96,128]{2,1,0:T(8,128)S(1)}, f32[4,96,128]{2,1,0:T(8,128)S(1)}, u32[]{:S(2)}, u32[]{:S(2)}) collective-permute-start(f32[4,96,128]{2,1,0:T(8,128)S(1)} %get-tuple-element.31), channel_id=1, source_target_pairs={{0,1},{1,0},{2,3},{3,2},{4,5},{5,4},{6,7},{7,6},{8,9},{9,8},{10,11... | collective-permute-start | bytes 589832 | tf_op jit(solution)/shard_map/ppermute | solution.py:657
  4.1 6.2 %collective-permute-start.1 = (f32[4,96,128]{2,1,0:T(8,128)S(1)}, f32[4,96,128]{2,1,0:T(8,128)S(1)}, u32[]{:S(2)}, u32[]{:S(2)}) collective-permute-start(f32[4,96,128]{2,1,0:T(8,128)S(1)} %get-tuple-element.32), channel_id=1, source_target_pairs={{0,16},{15,31},{16,0},{31,15},{1,2},{2,1},{3,4},{4,3},{5,6},{6,5},... | collective-permute-start | bytes 589832 | tf_op jit(solution)/shard_map/ppermute | solution.py:657
  11.5 2.8 %collective-permute-start.2 = (f32[2,128,128]{2,1,0:T(8,128)S(1)}, f32[2,128,128]{2,1,0:T(8,128)S(1)}, u32[]{:S(2)}, u32[]{:S(2)}) collective-permute-start(f32[2,128,128]{2,1,0:T(8,128)S(1)} %get-tuple-element.35), channel_id=1, source_target_pairs={{0,1},{1,0},{2,3},{3,2},{4,5},{5,4},{6,7},{7,6},{8,9},{9,8},{10,11... | collective-permute-start | bytes 393224 | tf_op jit(solution)/shard_map/ppermute | solution.py:657
  12.8 5.0 %collective-permute-start.3 = (f32[2,128,128]{2,1,0:T(8,128)S(1)}, f32[2,128,128]{2,1,0:T(8,128)S(1)}, u32[]{:S(2)}, u32[]{:S(2)}) collective-permute-start(f32[2,128,128]{2,1,0:T(8,128)S(1)} %get-tuple-element.36), channel_id=1, source_target_pairs={{0,16},{15,31},{16,0},{31,15},{1,2},{2,1},{3,4},{4,3},{5,6},{6,5},... | collective-permute-start | bytes 393224 | tf_op jit(solution)/shard_map/ppermute | solution.py:657
  32.4 4.4 %collective-permute-start.4 = (f32[8,2,8,128]{3,2,1,0:T(8,128)S(1)}, f32[8,2,8,128]{3,2,1,0:T(8,128)S(1)}, u32[]{:S(2)}, u32[]{:S(2)}) collective-permute-start(f32[8,2,8,128]{3,2,1,0:T(8,128)S(1)} %all_to_all.5.same_ref), channel_id=1, source_target_pairs={{0,1},{1,0},{2,3},{3,2},{4,5},{5,4},{6,7},{7,6},{8,9},{9,8},{10,11... | collective-permute-start | bytes 196616 | tf_op jit(solution)/shard_map/ppermute | solution.py:723
  32.4 3.0 %collective-permute-start.5 = (f32[2,32,128]{2,1,0:T(8,128)S(1)}, f32[2,32,128]{2,1,0:T(8,128)S(1)}, u32[]{:S(2)}, u32[]{:S(2)}) collective-permute-start(f32[2,32,128]{2,1,0:T(8,128)S(1)} %get-tuple-element.39), channel_id=1, source_target_pairs={{0,1},{1,0},{2,3},{3,2},{4,5},{5,4},{6,7},{7,6},{8,9},{9,8},{10,11... | collective-permute-start | bytes 98312 | tf_op jit(solution)/shard_map/ppermute | solution.py:719
  32.9 3.9 %collective-permute-start.6 = (f32[2,32,128]{2,1,0:T(8,128)S(1)}, f32[2,32,128]{2,1,0:T(8,128)S(1)}, u32[]{:S(2)}, u32[]{:S(2)}) collective-permute-start(f32[2,32,128]{2,1,0:T(8,128)S(1)} %get-tuple-element.40), channel_id=1, source_target_pairs={{0,16},{15,31},{16,0},{31,15},{1,2},{2,1},{3,4},{4,3},{5,6},{6,5},... | collective-permute-start | bytes 98312 | tf_op jit(solution)/shard_map/ppermute | solution.py:720
